TPU v7x, 512 devices: a whole 4x8x8 slice. The times are simulated.
512 devices in a mesh: dp: 2 (over core), expert: 32 (over y, x), tensor: 8 (over z).
Axes of the slice: x: 4, y: 8, z: 8, core: 2. Of those that a mesh axis runs over, the one named last changes fastest.
Arguments:
- tokens: bfloat16 [4096, 2048], P(('dp', 'expert'), 'tensor'), may hold values from -6 to 6
- expert_ids: int32 [4096, 6], P(('dp', 'expert')), may hold values from 0 to 31, all different within a row; in each aligned block of 64 rows (0 to 63, 64 to 127, ...) at most 16 rows name the same one
- route_weights: float32 [4096, 6], P(('dp', 'expert')), may hold values from 0.1 to 1
- w_gate: bfloat16 [32, 1408, 2048], P('expert', 'tensor'), may hold values from -0.125 to 0.125
- w_up: bfloat16 [32, 1408, 2048], P('expert', 'tensor'), may hold values from -0.125 to 0.125
- w_down: bfloat16 [32, 1408, 2048], P('expert', 'tensor'), may hold values from -0.15625 to 0.15625
- out_grad: bfloat16 [4096, 2048], P(('dp', 'expert'), 'tensor'), may hold values from -6 to 6
Outputs:
- layer_out: bfloat16 [4096, 2048], P(('dp', 'expert'), 'tensor')
- grad_tokens: bfloat16 [4096, 2048], P(('dp', 'expert'), 'tensor')
- grad_weights: float32 [4096, 6], P(('dp', 'expert'))
- grad_gate: bfloat16 [32, 1408, 2048], P('expert', 'tensor')
- grad_up: bfloat16 [32, 1408, 2048], P('expert', 'tensor')
- grad_down: bfloat16 [32, 1408, 2048], P('expert', 'tensor')
Inputs may be any that keep to these rules, and one draw needn't show every extreme that they name: `expert_ids`: each row names 6 different experts. In each aligned block of 64 rows no expert is named more than 16 times, a bound that some block reaches.
All inputs are finite; a program needn't handle non-finite values.
Results may differ from a plain program's by a relative error of at most 0.014.
Values may be sent and summed in bfloat16 or wider, within the bound.
No kernel may reach another device: no remote copies, remote signals or barrier semaphores. Data moves between devices by JAX's collectives and lax.ppermute only.
A program may use at most 128 MiB of HBM per device.

v0:
```python
import jax
import jax.numpy as jnp
from jax import lax
from jax.sharding import PartitionSpec as P


def build_slots(block_ids, capacity, experts):
    onehot = (block_ids[:, None] == jnp.arange(experts, dtype=jnp.int32)[None, :]).astype(jnp.int32)
    before = jnp.cumsum(onehot, axis=0) - onehot
    position = jnp.sum(before * onehot, axis=1)
    slot_index = block_ids * capacity + position
    count = block_ids.shape[0]
    lookup = (
        jnp.full((experts * capacity,), -1, jnp.int32)
        .at[slot_index]
        .set(jnp.arange(count, dtype=jnp.int32))
    )
    return (slot_index, lookup)


def rounded(value):
    return lax.optimization_barrier(value.astype(jnp.bfloat16)).astype(jnp.float32)


def contract_rows(left, right):
    return lax.dot_general(
        left, right, (((0,), (0,)), ((), ())), preferred_element_type=jnp.float32
    )


def contract_cols(left, right):
    return lax.dot_general(
        left, right, (((1,), (1,)), ((), ())), preferred_element_type=jnp.float32
    )


def bring_back(part, slot_rows, scales, direction):
    summed = lax.psum_scatter(
        lax.optimization_barrier(part).astype(jnp.float32).astype(jnp.bfloat16),
        "tensor",
        scatter_dimension=1,
        tiled=True,
    ).astype(jnp.float32)
    returned = lax.all_to_all(
        summed.astype(jnp.bfloat16), "expert", split_axis=0, concat_axis=0, tiled=True
    ).astype(summed.dtype)
    picked = jnp.take(returned, slot_rows, axis=0)
    if scales is None:
        total = jnp.sum(picked, axis=1)
    else:
        total = jnp.sum(scales[:, :, None] * picked, axis=1)
    dots = None
    if direction is not None:
        dots = jnp.sum(direction.astype(jnp.float32)[:, None, :] * picked, axis=2)
    return (total, dots)


def body(tokens, expert_ids, route_weights, w_gate, w_up, w_down, out_grad):
    experts = lax.axis_size("expert")
    tok_rows, choose = expert_ids.shape
    capacity = tok_rows * 8 // experts
    slot_index, lookup = build_slots(expert_ids.reshape(-1), capacity, experts)
    filled = lookup >= 0
    pair_index = jnp.where(filled, lookup, 0)
    source_row = jnp.where(filled, pair_index // choose, tok_rows)
    slot_weight = jnp.where(
        filled, route_weights.reshape(-1)[pair_index], jnp.zeros((), jnp.float32)
    )
    slot_rows = slot_index.reshape(tok_rows, choose)

    def select_rows(rows):
        padded = jnp.concatenate([rows, jnp.zeros((1, rows.shape[1]), rows.dtype)], axis=0)
        return jnp.take(padded, source_row, axis=0)

    gathered, gathered_dy = (
        lax.all_gather(tokens, "tensor", axis=1, tiled=True),
        lax.all_gather(out_grad, "tensor", axis=1, tiled=True),
    )
    sent_rows = select_rows(gathered)
    sent_grads = (slot_weight[:, None] * select_rows(gathered_dy).astype(jnp.float32)).astype(
        jnp.bfloat16
    )
    sent_rows, sent_grads = (sent_rows, sent_grads)
    expert_rows, expert_grads = (
        lax.all_to_all(sent_rows, "expert", split_axis=0, concat_axis=0, tiled=True),
        lax.all_to_all(sent_grads, "expert", split_axis=0, concat_axis=0, tiled=True),
    )
    gate_matrix = w_gate[0]
    up_matrix = w_up[0]
    down_matrix = w_down[0]
    gate_value = contract_cols(expert_rows, gate_matrix)
    up_value = contract_cols(expert_rows, up_matrix)
    hidden = (jax.nn.silu(gate_value) * up_value).astype(jnp.bfloat16)
    part = jnp.dot(hidden, down_matrix, preferred_element_type=jnp.float32).astype(jnp.bfloat16)
    grad_hidden = contract_cols(expert_grads, down_matrix)
    sigma = jax.nn.sigmoid(gate_value)
    gate_rows = (grad_hidden * up_value * sigma * (1.0 + gate_value * (1.0 - sigma))).astype(
        jnp.bfloat16
    )
    up_rows = (grad_hidden * jax.nn.silu(gate_value)).astype(jnp.bfloat16)
    grad_part = (
        jnp.dot(gate_rows, gate_matrix, preferred_element_type=jnp.float32)
        + jnp.dot(up_rows, up_matrix, preferred_element_type=jnp.float32)
    ).astype(jnp.bfloat16)
    gate_term = rounded(contract_rows(gate_rows, expert_rows))
    up_term = rounded(contract_rows(up_rows, expert_rows))
    down_term = rounded(contract_rows(hidden, expert_grads))
    gate_sum, up_sum, down_sum = (
        lax.psum(gate_term.astype(jnp.bfloat16), "dp").astype(jnp.float32),
        lax.psum(up_term.astype(jnp.bfloat16), "dp").astype(jnp.float32),
        lax.psum(down_term.astype(jnp.bfloat16), "dp").astype(jnp.float32),
    )
    layer_total, dots = bring_back(part, slot_rows, route_weights, out_grad)
    grad_total, nothing = bring_back(grad_part, slot_rows, None, None)
    weight_dots = lax.psum(dots, "tensor")
    return (
        layer_total.astype(jnp.bfloat16),
        grad_total.astype(jnp.bfloat16),
        weight_dots,
        gate_sum.astype(jnp.bfloat16)[None],
        up_sum.astype(jnp.bfloat16)[None],
        down_sum.astype(jnp.bfloat16)[None],
    )


def solution(mesh):
    placed = (
        P(("dp", "expert"), "tensor"),
        P(("dp", "expert"), None),
        P(("dp", "expert"), None),
        P("expert", "tensor", None),
        P("expert", "tensor", None),
        P("expert", "tensor", None),
        P(("dp", "expert"), "tensor"),
    )
    return jax.shard_map(
        body,
        mesh=mesh,
        in_specs=placed,
        out_specs=(
            P(("dp", "expert"), "tensor"),
            P(("dp", "expert"), "tensor"),
            P(("dp", "expert"), None),
            P("expert", "tensor", None),
            P("expert", "tensor", None),
            P("expert", "tensor", None),
        ),
        check_vma=False,
    )
```

profile of v0, /device:TPU:8, one launch (start us, length us, event | category | flops | bytes accessed | tf_op | source)
XLA Modules:
  0.0 312.5 jit_solution(13329957115378280598)
XLA Ops:
  11.4 2.9 scatter_custom_fusion
  14.3 31.4 %all_gather.6 = bf16[64,2048]{1,0:T(8,128)(2,1)S(1)} all-gather(bf16[64,256]{1,0:T(8,128)(2,1)} %param.11), channel_id=1, replica_groups=mesh['dp'=2,'expert'=32,'tensor'=8] {'tensor'}, dimensions={1}, use_global_device_ids=true | all-gather | bytes 294912 | tf_op jit(solution)/shard_map/all_gather | solution.py:76
  45.7 2.5 gather_fusion.1
  49.8 10.3 %all-to-all-start = ((bf16[32,16,2048]{2,1,0:T(8,128)(2,1)}), bf16[32,16,2048]{2,1,0:T(8,128)(2,1)S(1)}, u32[]{:S(2)}, u32[]{:S(2)}) async-start(bf16[32,16,2048]{2,1,0:T(8,128)(2,1)} %bitcast.68), calls=%async_computation | async-start | bytes 4194304 | tf_op jit(solution)/shard_map/all_to_all | solution.py:85
  60.8 24.8 %all_gather.7 = bf16[64,2048]{1,0:T(8,128)(2,1)S(1)} all-gather(bf16[64,256]{1,0:T(8,128)(2,1)S(1)} %copy-done.8), channel_id=1, replica_groups=mesh['dp'=2,'expert'=32,'tensor'=8] {'tensor'}, dimensions={1}, use_global_device_ids=true | all-gather | bytes 294912 | tf_op jit(solution)/shard_map/all_gather | solution.py:77
  85.6 3.3 %gather_fusion.3 = bf16[512,2048]{1,0:T(8,128)(2,1)} fusion(bf16[65,2048]{1,0:T(8,128)(2,1)S(1)} %concatenate.7, s32[1024]{0:T(1024)S(1)} %pad_clamp_fusion.2), kind=kCustom, calls=%fused_computation.2.clone | custom fusion | bytes 4196352 | tf_op jit(solution)/shard_map/jit(_take)/gather | solution.py:73
  88.9 3.5 %gather_fusion = f32[512]{0:T(512)S(1)} fusion(f32[384]{0:T(512)S(1)} %reshape.89, s32[1024]{0:T(1024)S(1)} %pad_clamp_fusion), kind=kCustom, calls=%fused_computation.4 | custom fusion | bytes 6144 | tf_op jit(solution)/shard_map/gather | solution.py:67
  92.5 3.4 %multiply_convert_fusion = bf16[512,2048]{1,0:T(8,128)(2,1)} fusion(bf16[512,2048]{1,0:T(8,128)(2,1)} %gather_fusion.3, f32[512]{0:T(512)S(1)} %broadcast_select_fusion.1, pred[512]{0:T(512)(128)(4,1)S(1)} %get-tuple-element.28), kind=kLoop, calls=%fused_computation.7 | loop fusion | flops 4194304 | bytes 4196864 | tf_op jit(solution)/shard_map/convert_element_type | solution.py:80
  95.9 7.8 %all-to-all-done = bf16[32,16,2048]{2,1,0:T(8,128)(2,1)S(1)} async-done(((bf16[32,16,2048]{2,1,0:T(8,128)(2,1)}), bf16[32,16,2048]{2,1,0:T(8,128)(2,1)S(1)}, u32[]{:S(2)}, u32[]{:S(2)}) %all-to-all-start) | async-done | bytes 2097184 | tf_op jit(solution)/shard_map/all_to_all | solution.py:85
  103.7 6.6 %all-to-all-start.2 = ((bf16[32,16,2048]{2,1,0:T(8,128)(2,1)}), bf16[32,16,2048]{2,1,0:T(8,128)(2,1)}, u32[]{:S(2)}, u32[]{:S(2)}) async-start(bf16[32,16,2048]{2,1,0:T(8,128)(2,1)} %bitcast.69), calls=%async_computation.3 | async-start | bytes 4194304 | tf_op jit(solution)/shard_map/all_to_all | solution.py:86
  113.6 40.8 %all-to-all-done.2 = bf16[32,16,2048]{2,1,0:T(8,128)(2,1)} async-done(((bf16[32,16,2048]{2,1,0:T(8,128)(2,1)}), bf16[32,16,2048]{2,1,0:T(8,128)(2,1)}, u32[]{:S(2)}, u32[]{:S(2)}) %all-to-all-start.2) | async-done | bytes 2097184 | tf_op jit(solution)/shard_map/all_to_all | solution.py:86
  154.5 2.7 multiply_convert_fusion.1
  158.3 2.1 add_convert_fusion
  160.5 2.0 convolution_convert_fusion
  162.8 3.0 convolution_convert_fusion.1
  168.6 31.9 %reduce-scatter.5.cloned.1.call-done = bf16[512,256]{1,0:T(8,128)(2,1)} async-done(((bf16[512,2048]{1,0:T(8,128)(2,1)}), bf16[512,256]{1,0:T(8,128)(2,1)}) %reduce-scatter.5.cloned.1.call-update) | async-done | bytes 262160 | tf_op jit(solution)/shard_map/reduce_scatter | solution.py:38
  200.6 9.9 %all-to-all-start.3 = ((bf16[32,16,256]{2,1,0:T(8,128)(2,1)}), bf16[32,16,256]{2,1,0:T(8,128)(2,1)S(1)}, u32[]{:S(2)}, u32[]{:S(2)}) async-start(bf16[32,16,256]{2,1,0:T(8,128)(2,1)} %bitcast.74), calls=%async_computation.5 | async-start | bytes 524288 | tf_op jit(solution)/shard_map/all_to_all | solution.py:44
  210.7 37.0 %reduce-scatter.3.cloned.1.call-done = bf16[512,256]{1,0:T(8,128)(2,1)} async-done(((bf16[512,2048]{1,0:T(8,128)(2,1)}), bf16[512,256]{1,0:T(8,128)(2,1)}) %reduce-scatter.3.cloned.1.call-update) | async-done | bytes 262160 | tf_op jit(solution)/shard_map/reduce_scatter | solution.py:38
  247.7 10.1 %all-to-all-start.1 = ((bf16[32,16,256]{2,1,0:T(8,128)(2,1)}), bf16[32,16,256]{2,1,0:T(8,128)(2,1)S(1)}, u32[]{:S(2)}, u32[]{:S(2)}) async-start(bf16[32,16,256]{2,1,0:T(8,128)(2,1)} %bitcast.73), calls=%async_computation.2 | async-start | bytes 524288 | tf_op jit(solution)/shard_map/all_to_all | solution.py:44
  258.2 1.7 gather_fusion.4
  260.0 8.6 %all-to-all-done.1 = bf16[32,16,256]{2,1,0:T(8,128)(2,1)S(1)} async-done(((bf16[32,16,256]{2,1,0:T(8,128)(2,1)}), bf16[32,16,256]{2,1,0:T(8,128)(2,1)S(1)}, u32[]{:S(2)}, u32[]{:S(2)}) %all-to-all-start.1) | async-done | bytes 262176 | tf_op jit(solution)/shard_map/all_to_all | solution.py:44
  271.5 27.9 %psum.28 = f32[64,6]{1,0:T(8,128)S(1)} all-reduce(f32[64,6]{1,0:T(8,128)S(1)} %get-tuple-element.20), channel_id=1, replica_groups=mesh['dp'=2,'expert'=32,'tensor'=8] {'tensor'}, use_global_device_ids=true, to_apply=%region_9.12 | all-reduce | flops 384 | bytes 3072 | tf_op jit(solution)/shard_map/psum | solution.py:115
  300.0 2.1 copy.46
  302.1 2.0 copy.47
  (76 shorter events, 18.3 us)
Async XLA Ops:
  8.0 146.5 %copy-start = (bf16[1,176,2048]{2,1,0:T(8,128)(2,1)S(1)}, bf16[1,176,2048]{2,1,0:T(8,128)(2,1)}, u32[]{:S(2)}) copy-start(bf16[1,176,2048]{2,1,0:T(8,128)(2,1)} %param.16) | copy-start | bytes 2162692
  49.8 10.3 %copy-start.11 = (f32[64,6]{0,1:T(8,128)S(1)}, f32[64,6]{0,1:T(8,128)}, u32[]{:S(2)}) copy-start(f32[64,6]{0,1:T(8,128)} %param.13) | copy-start | bytes 4612
  49.8 11.0 %copy-start.8 = (bf16[64,256]{1,0:T(8,128)(2,1)S(1)}, bf16[64,256]{1,0:T(8,128)(2,1)}, u32[]{:S(2)}) copy-start(bf16[64,256]{1,0:T(8,128)(2,1)} %param.17) | copy-start | bytes 98308
  49.8 53.9 %all-to-all-start = ((bf16[32,16,2048]{2,1,0:T(8,128)(2,1)}), bf16[32,16,2048]{2,1,0:T(8,128)(2,1)S(1)}, u32[]{:S(2)}, u32[]{:S(2)}) async-start(bf16[32,16,2048]{2,1,0:T(8,128)(2,1)} %bitcast.68), calls=%async_computation | async-start | bytes 4194304 | tf_op jit(solution)/shard_map/all_to_all | solution.py:85
  60.2 0.6 copy-start.6
  103.7 6.7 %copy-start.3 = (bf16[1,176,2048]{2,1,0:T(8,128)(2,1)S(1)}, bf16[1,176,2048]{2,1,0:T(8,128)(2,1)}, u32[]{:S(2)}) copy-start(bf16[1,176,2048]{2,1,0:T(8,128)(2,1)} %param.15) | copy-start | bytes 2162692
  103.7 50.7 %all-to-all-start.2 = ((bf16[32,16,2048]{2,1,0:T(8,128)(2,1)}), bf16[32,16,2048]{2,1,0:T(8,128)(2,1)}, u32[]{:S(2)}, u32[]{:S(2)}) async-start(bf16[32,16,2048]{2,1,0:T(8,128)(2,1)} %bitcast.69), calls=%async_computation.3 | async-start | bytes 4194304 | tf_op jit(solution)/shard_map/all_to_all | solution.py:86
  110.4 90.2 %reduce-scatter.5.cloned.1.call-start = ((), (), s32[]{:S(2)}) async-start(), calls=%async_computation.7 | async-start | bytes 2359296 | tf_op jit(solution)/shard_map/reduce_scatter | solution.py:38
  110.4 1.6 copy-start.1
  154.5 2.7 copy-start.2
  157.2 1.1 copy-start.4
  160.4 87.2 %reduce-scatter.3.cloned.1.call-start = ((), (), s32[]{:S(2)}) async-start(), calls=%async_computation.6 | async-start | bytes 2359296 | tf_op jit(solution)/shard_map/reduce_scatter | solution.py:38
  162.6 137.4 %all-reduce.5.cloned.1.call-start = ((), (), s32[]{:S(2)}) async-start(), calls=%async_computation.8 | async-start | bytes 4325376 | tf_op jit(solution)/shard_map/psum | solution.py:109
  168.6 42.0 %copy-start.9 = (bf16[64,256]{1,0:T(8,128)(2,1)S(1)}, bf16[64,256]{1,0:T(8,128)(2,1)}, u32[]{:S(2)}) copy-start(bf16[64,256]{1,0:T(8,128)(2,1)} %param.17) | copy-start | bytes 98308
  168.6 89.2 %copy-start.10 = (s32[64,6]{0,1:T(8,128)S(1)}, s32[64,6]{0,1:T(8,128)}, u32[]{:S(2)}) copy-start(s32[64,6]{0,1:T(8,128)} %param.12) | copy-start | bytes 4612
  200.6 47.1 %all-to-all-start.3 = ((bf16[32,16,256]{2,1,0:T(8,128)(2,1)}), bf16[32,16,256]{2,1,0:T(8,128)(2,1)S(1)}, u32[]{:S(2)}, u32[]{:S(2)}) async-start(bf16[32,16,256]{2,1,0:T(8,128)(2,1)} %bitcast.74), calls=%async_computation.5 | async-start | bytes 524288 | tf_op jit(solution)/shard_map/all_to_all | solution.py:44
  247.7 20.9 %all-to-all-start.1 = ((bf16[32,16,256]{2,1,0:T(8,128)(2,1)}), bf16[32,16,256]{2,1,0:T(8,128)(2,1)S(1)}, u32[]{:S(2)}, u32[]{:S(2)}) async-start(bf16[32,16,256]{2,1,0:T(8,128)(2,1)} %bitcast.73), calls=%async_computation.2 | async-start | bytes 524288 | tf_op jit(solution)/shard_map/all_to_all | solution.py:44
  268.6 1.8 copy-start.7
  300.0 4.2 %copy-start.5 = (bf16[1,176,2048]{2,1,0:T(8,128)(2,1)S(1)}, bf16[1,176,2048]{2,1,0:T(8,128)(2,1)}, u32[]{:S(2)}) copy-start(bf16[1,176,2048]{2,1,0:T(8,128)(2,1)} %get-tuple-element.38) | copy-start | bytes 2162692
Sparse Core Ops, SparseCore 0:
  160.6 39.9 reduce-scatter.4
  203.4 44.1 reduce-scatter.2
Sparse Core Ops, SparseCore 1:
  168.7 31.7 all-reduce.4
where the time goes:
time: 313 us; the launch traced here: 312 us
  waiting for transfers between devices  126 us (40%)
  blocking collectives  84 us (27%)
  starting transfers between devices  37.2 us (12%)
  local copies, waits for them, and re-layouts  24.6 us (8%)
  matrix products  16.6 us (5%)
  between operations  15.8 us (5%)
  other arithmetic  8.07 us (3%)
    reduce_scatter x2, waiting for transfers between devices, bring_back(): lax.psum_scatter(lax.optimization_barrier(part).astype(jnp.float32).astyp...  68.9 us
    all_to_all x1, waiting for transfers between devices, body(): lax.all_to_all(sent_grads, 'expert', split_axis=0, concat_axis=0, tiled=T...  40.8 us
    all_gather x1, blocking collectives, body(): lax.all_gather(tokens, 'tensor', axis=1, tiled=True)  31.4 us
    psum x1, blocking collectives, body(): weight_dots = lax.psum(dots, 'tensor')  27.9 us
    all_gather x1, blocking collectives, body(): lax.all_gather(out_grad, 'tensor', axis=1, tiled=True)  24.8 us
    all_to_all x2, starting transfers between devices, bring_back(): lax.all_to_all(summed.astype(jnp.bfloat16), 'expert', split_axis=0, conca...  20 us
    all_to_all x1, starting transfers between devices, body(): lax.all_to_all(sent_rows, 'expert', split_axis=0, concat_axis=0, tiled=True)  10.3 us
    all_to_all x2, waiting for transfers between devices, bring_back(): lax.all_to_all(summed.astype(jnp.bfloat16), 'expert', split_axis=0, conca...  8.59 us
  transfers between devices with their start and end apart: 7, of which 5 were waited for; matrix products, arithmetic and copies ran while one was open for 9% of the time, Pallas kernels for 0%

commit v1 on v0

v1 whole, which is shorter than its diff:
```python
import jax
import jax.numpy as jnp
from jax import lax
from jax.experimental import pallas as pl
from jax.experimental.pallas import tpu as pltpu
from jax.sharding import PartitionSpec as P

BF = jnp.bfloat16
F32 = jnp.float32
N_T = 8


def nt(left, right):
    return lax.dot_general(left, right, (((1,), (1,)), ((), ())), preferred_element_type=F32)


def tn(left, right):
    return lax.dot_general(left, right, (((0,), (0,)), ((), ())), preferred_element_type=F32)


def nn(left, right):
    return lax.dot_general(left, right, (((1,), (0,)), ((), ())), preferred_element_type=F32)


def shift(x, by):
    return lax.ppermute(x, "tensor", [(i, (i + by) % N_T) for i in range(N_T)])


def gather_ring(x, g):
    xs, gs = [x] + [None] * (N_T - 1), [g] + [None] * (N_T - 1)
    half = N_T // 2
    for s in range(1, half + 1):
        xs[-s] = shift(xs[(1 - s) % N_T], 1)
        gs[-s if s < half else s] = shift(gs[(1 - s) % N_T], 1) if s < half else shift(gs[s - 1], -1)
        if s < half:
            xs[s] = shift(xs[s - 1], -1)
            gs[s] = shift(gs[s - 1], -1)
    return xs, gs


def reduce_ring(terms, up, down):
    u, d = terms[up], terms[-down % N_T]
    for s in range(1, max(up, down) + 1):
        if s <= up:
            u = shift(u, 1)
            if s < up:
                u = (u.astype(F32) + terms[up - s].astype(F32)).astype(BF)
        if s <= down:
            d = shift(d, -1)
            if s < down:
                d = (d.astype(F32) + terms[(s - down) % N_T].astype(F32)).astype(BF)
    return (terms[0].astype(F32) + u.astype(F32) + d.astype(F32)).astype(BF)


def expert_kernel(meta, *refs):
    xs, gs = refs[:N_T], refs[N_T : 2 * N_T]
    wg, wu, wd, part, gpart, gout, uout, dout = refs[2 * N_T :]
    z = meta[0]
    rows, width = xs[0].shape

    def col(places):
        at = (z + places) & (N_T - 1)
        return pl.ds(pl.multiple_of(at * width, width), width)

    gate_value = nt(xs[0][...], wg[:, col(0)])
    up_value = nt(xs[0][...], wu[:, col(0)])
    grad_hidden = nt(gs[0][...], wd[:, col(0)])
    for s in range(1, N_T):
        gate_value += nt(xs[s][...], wg[:, col(s)])
        up_value += nt(xs[s][...], wu[:, col(s)])
        grad_hidden += nt(gs[s][...], wd[:, col(s)])
    sigma = jax.nn.sigmoid(gate_value)
    silu = gate_value * sigma
    hidden = (silu * up_value).astype(BF)
    gate_rows = (grad_hidden * up_value * sigma * (1.0 + gate_value * (1.0 - sigma))).astype(BF)
    up_rows = (grad_hidden * silu).astype(BF)

    product = hidden.astype(F32) * grad_hidden
    high = product.astype(BF)
    low = (product - high.astype(F32)).astype(BF)
    ones = jnp.ones((8, product.shape[1]), BF)
    dots = nt(ones, high) + nt(ones, low)
    line = lax.broadcasted_iota(jnp.int32, (8, width), 0)
    dots = jnp.where(line < 4, dots[:, :width], dots[:, width:]).astype(BF)
    for d in range(N_T - 1, -1, -1):
        part[d, :rows] = nn(hidden, wd[:, col(d)]).astype(BF)
        part[d, rows:] = dots
        gpart[d] = (nn(gate_rows, wg[:, col(d)]) + nn(up_rows, wu[:, col(d)])).astype(BF)
    for s in range(N_T):
        gout[:, col(s)] = tn(gate_rows, xs[s][...]).astype(BF)
        uout[:, col(s)] = tn(up_rows, xs[s][...]).astype(BF)
        dout[:, col(s)] = tn(hidden, gs[s][...]).astype(BF)


def expert_work(meta, xs, gs, wg, wu, wd):
    rows, width = xs[0].shape
    vmem = pl.BlockSpec(memory_space=pltpu.VMEM)
    grad = jax.ShapeDtypeStruct(wg.shape, BF)
    return pl.pallas_call(
        expert_kernel,
        out_shape=(
            jax.ShapeDtypeStruct((N_T, rows + 8, width), BF),
            jax.ShapeDtypeStruct((N_T, rows, width), BF),
            grad, grad, grad,
        ),
        in_specs=[pl.BlockSpec(memory_space=pltpu.SMEM)] + [vmem] * (2 * N_T + 3),
        out_specs=(vmem,) * 5,
        name="expert",
    )(meta, *xs, *gs, wg, wu, wd)


def body(tokens, expert_ids, route_weights, w_gate, w_up, w_down, out_grad):
    experts = lax.axis_size("expert")
    tok_rows, choose = expert_ids.shape
    width = tokens.shape[1]
    cap = tok_rows * 8 // experts
    slots = experts * cap
    z = lax.axis_index("tensor")

    ids_t = expert_ids.T
    hit = ids_t[:, None, :] == jnp.arange(experts, dtype=jnp.int32)[None, :, None]
    named = jnp.any(hit, axis=0)
    weight_et = jnp.sum(jnp.where(hit, route_weights.T[:, None, :], 0.0), axis=0)
    earlier = jnp.arange(tok_rows)[:, None] < jnp.arange(tok_rows)[None, :]
    place = nn(named.astype(BF), earlier.astype(BF))
    chosen = named[:, None, :] & (
        place[:, None, :] == jnp.arange(cap, dtype=F32)[None, :, None]
    )
    pick = chosen.reshape(slots, tok_rows).astype(BF)
    pick_w = jnp.where(chosen, weight_et[:, None, :], 0.0)
    slot_w = jnp.sum(pick_w, axis=2).reshape(slots)
    pick_w = pick_w.reshape(slots, tok_rows)

    rows = nn(pick, tokens).astype(BF)
    grads = (slot_w[:, None] * nn(pick, out_grad)).astype(BF)
    sent = jnp.concatenate(
        [rows.reshape(experts, cap, width), grads.reshape(experts, cap, width)], axis=1
    )
    got = lax.all_to_all(sent, "expert", split_axis=0, concat_axis=0, tiled=True)
    x0 = got[:, :cap].reshape(slots, width)
    g0 = got[:, cap:].reshape(slots, width)

    xs, gs = gather_ring(x0, g0)
    meta = z.astype(jnp.int32).reshape(1)
    part, gpart, gate_term, up_term, down_term = expert_work(
        meta, xs, gs, w_gate[0], w_up[0], w_down[0]
    )

    p = reduce_ring(part, N_T // 2, N_T // 2 - 1)
    g = reduce_ring(gpart, N_T // 2 - 1, N_T // 2)
    back, grad_back = p[:slots], g
    dots = p[slots:]
    slot_dots = jnp.concatenate([dots[0], dots[4]]).reshape(experts, cap)

    def over_dp(term):
        other = lax.ppermute(term, "dp", [(0, 1), (1, 0)])
        return (term.astype(F32) + other.astype(F32)).astype(BF)[None]

    gate_grad, up_grad, down_grad = over_dp(gate_term), over_dp(up_term), over_dp(down_term)

    extra = jnp.pad(slot_dots[:, None, :], ((0, 0), (0, 7), (0, width - cap)))
    sent = jnp.concatenate(
        [back.reshape(experts, cap, width), grad_back.reshape(experts, cap, width), extra], axis=1
    )
    got = lax.all_to_all(sent, "expert", split_axis=0, concat_axis=0, tiled=True)
    home = got[:, :cap].reshape(slots, width)
    grad_home = got[:, cap : 2 * cap].reshape(slots, width)
    slot_dots = got[:, 2 * cap, :cap].astype(F32)

    layer = lax.dot_general(
        pick_w, home.astype(F32), (((0,), (0,)), ((), ())),
        precision=lax.Precision.HIGHEST, preferred_element_type=F32,
    )
    grad_tok = tn(pick, grad_home)
    dots_et = jnp.sum(jnp.where(chosen, slot_dots[:, :, None], 0.0), axis=1)
    dots_kt = jnp.sum(jnp.where(hit, dots_et[None], 0.0), axis=1)
    grad_w = dots_kt.T / route_weights
    return layer.astype(BF), grad_tok.astype(BF), grad_w, gate_grad, up_grad, down_grad


def solution(mesh):
    placed = (
        P(("dp", "expert"), "tensor"),
        P(("dp", "expert"), None),
        P(("dp", "expert"), None),
        P("expert", "tensor", None),
        P("expert", "tensor", None),
        P("expert", "tensor", None),
        P(("dp", "expert"), "tensor"),
    )
    return jax.shard_map(
        body,
        mesh=mesh,
        in_specs=placed,
        out_specs=(
            P(("dp", "expert"), "tensor"),
            P(("dp", "expert"), "tensor"),
            P(("dp", "expert"), None),
            P("expert", "tensor", None),
            P("expert", "tensor", None),
            P("expert", "tensor", None),
        ),
        check_vma=False,
    )
```

time: 313 us -> 195 us (0.62)
  the two profiles are of different devices: /device:TPU:8 before, /device:TPU:1 now
where the time goes in v1:
time: 195 us; the launch traced here: 194 us
  starting transfers between devices  115 us (59%)
  blocking collectives  26.6 us (14%)
  waiting for transfers between devices  18 us (9%)
  other arithmetic  14.8 us (8%)
  Pallas kernels  10.4 us (5%)
  matrix products  5.06 us (3%)
  local copies, waits for them, and re-layouts  2.8 us (1%)
    ppermute x28, starting transfers between devices, shift(): return lax.ppermute(x, 'tensor', [(i, (i + by) % N_T) for i in range(N_T)])  92.1 us
    all_to_all x1, blocking collectives, body(): lax.all_to_all(sent, 'expert', split_axis=0, concat_axis=0, tiled=True)  26.6 us
    ppermute x3, starting transfers between devices, over_dp(): other = lax.ppermute(term, 'dp', [(0, 1), (1, 0)])  18 us
    all_to_all x1, waiting for transfers between devices, body(): lax.all_to_all(sent, 'expert', split_axis=0, concat_axis=0, tiled=True)  13.9 us
    pallas_call x1, Pallas kernels, expert_work(): pl.pallas_call(expert_kernel, out_shape=(jax.ShapeDtypeStruct((N_T, rows...  10.4 us
    broadcast_in_dim x3, other arithmetic, over_dp(): return (term.astype(F32) + other.astype(F32)).astype(BF)[None]  5.53 us
    all_to_all x1, starting transfers between devices, body(): lax.all_to_all(sent, 'expert', split_axis=0, concat_axis=0, tiled=True)  4.61 us
    ppermute x28, waiting for transfers between devices, shift(): return lax.ppermute(x, 'tensor', [(i, (i + by) % N_T) for i in range(N_T)])  4.1 us
  transfers between devices with their start and end apart: 32, of which 3 were waited for; matrix products, arithmetic and copies ran while one was open for 7% of the time, Pallas kernels for 0%

profile of v1, /device:TPU:1, one launch (start us, length us, event | category | flops | bytes accessed | tf_op | source)
XLA Modules:
  0.0 193.8 jit_solution(16641811835806728741)
XLA Ops:
  4.0 26.6 %all_to_all.10 = bf16[32,32,256]{2,1,0:T(8,128)(2,1)S(1)} all-to-all(bf16[32,32,256]{2,1,0:T(8,128)(2,1)S(1)} %pad_maximum_fusion.1), channel_id=1, replica_groups=mesh['dp'=2,'expert'=32,'tensor'=8] {'expert'}, dimensions={0} | all-to-all | bytes 1048576 | tf_op jit(solution)/shard_map/all_to_all | solution.py:139
  30.6 4.0 %collective-permute-start.3 = (bf16[512,256]{1,0:T(8,128)(2,1)S(1)}, bf16[512,256]{1,0:T(8,128)(2,1)S(1)}, u32[]{:S(2)}, u32[]{:S(2)}) collective-permute-start(bf16[512,256]{1,0:T(8,128)(2,1)S(1)} %bitcast.88), channel_id=1, source_target_pairs={{0,1},{1,2},{2,3},{3,4},{4,5},{5,6},{6,7},{7,0},{8,9},{9,10},{10,1... | collective-permute-start | bytes 786440 | tf_op jit(solution)/shard_map/ppermute | solution.py:26
  34.6 8.6 %collective-permute-start.7 = (bf16[512,256]{1,0:T(8,128)(2,1)S(1)}, bf16[512,256]{1,0:T(8,128)(2,1)S(1)}, u32[]{:S(2)}, u32[]{:S(2)}) collective-permute-start(bf16[512,256]{1,0:T(8,128)(2,1)S(1)} %bitcast.85), channel_id=1, source_target_pairs={{0,7},{1,0},{2,1},{3,2},{4,3},{5,4},{6,5},{7,6},{8,15},{9,8},{10,9... | collective-permute-start | bytes 786440 | tf_op jit(solution)/shard_map/ppermute | solution.py:26
  43.2 3.4 %collective-permute-start = (bf16[512,256]{1,0:T(8,128)(2,1)S(1)}, bf16[512,256]{1,0:T(8,128)(2,1)S(1)}, u32[]{:S(2)}, u32[]{:S(2)}) collective-permute-start(bf16[512,256]{1,0:T(8,128)(2,1)S(1)} %bitcast.89), channel_id=1, source_target_pairs={{0,7},{1,0},{2,1},{3,2},{4,3},{5,4},{6,5},{7,6},{8,15},{9,8},{10,9... | collective-permute-start | bytes 786440 | tf_op jit(solution)/shard_map/ppermute | solution.py:26
  50.5 4.6 %collective-permute-start.8 = (bf16[512,256]{1,0:T(8,128)(2,1)S(1)}, bf16[512,256]{1,0:T(8,128)(2,1)S(1)}, u32[]{:S(2)}, u32[]{:S(2)}) collective-permute-start(bf16[512,256]{1,0:T(8,128)(2,1)S(1)} %collective-permute-done.7.refs_9_), channel_id=1, source_target_pairs={{0,7},{1,0},{2,1},{3,2},{4,3},{5,4},{6,5},{7,6},{8,15},{9,8},{10,9... | collective-permute-start | bytes 786440 | tf_op jit(solution)/shard_map/ppermute | solution.py:26
  55.1 3.4 %collective-permute-start.1 = (bf16[512,256]{1,0:T(8,128)(2,1)S(1)}, bf16[512,256]{1,0:T(8,128)(2,1)S(1)}, u32[]{:S(2)}, u32[]{:S(2)}) collective-permute-start(bf16[512,256]{1,0:T(8,128)(2,1)S(1)} %collective-permute-done.refs_1_), channel_id=1, source_target_pairs={{0,7},{1,0},{2,1},{3,2},{4,3},{5,4},{6,5},{7,6},{8,15},{9,8},{10,9... | collective-permute-start | bytes 786440 | tf_op jit(solution)/shard_map/ppermute | solution.py:26
  62.4 4.6 %collective-permute-start.9 = (bf16[512,256]{1,0:T(8,128)(2,1)S(1)}, bf16[512,256]{1,0:T(8,128)(2,1)S(1)}, u32[]{:S(2)}, u32[]{:S(2)}) collective-permute-start(bf16[512,256]{1,0:T(8,128)(2,1)S(1)} %collective-permute-done.8.refs_10_), channel_id=1, source_target_pairs={{0,7},{1,0},{2,1},{3,2},{4,3},{5,4},{6,5},{7,6},{8,15},{9,8},{10,9... | collective-permute-start | bytes 786440 | tf_op jit(solution)/shard_map/ppermute | solution.py:26
  67.0 3.4 %collective-permute-start.2 = (bf16[512,256]{1,0:T(8,128)(2,1)S(1)}, bf16[512,256]{1,0:T(8,128)(2,1)S(1)}, u32[]{:S(2)}, u32[]{:S(2)}) collective-permute-start(bf16[512,256]{1,0:T(8,128)(2,1)S(1)} %collective-permute-done.1.refs_2_), channel_id=1, source_target_pairs={{0,7},{1,0},{2,1},{3,2},{4,3},{5,4},{6,5},{7,6},{8,15},{9,8},{10,9... | collective-permute-start | bytes 786440 | tf_op jit(solution)/shard_map/ppermute | solution.py:26
  74.2 4.6 %collective-permute-start.10 = (bf16[512,256]{1,0:T(8,128)(2,1)S(1)}, bf16[512,256]{1,0:T(8,128)(2,1)}, u32[]{:S(2)}, u32[]{:S(2)}) collective-permute-start(bf16[512,256]{1,0:T(8,128)(2,1)S(1)} %collective-permute-done.9.refs_11_), channel_id=1, source_target_pairs={{0,7},{1,0},{2,1},{3,2},{4,3},{5,4},{6,5},{7,6},{8,15},{9,8},{10,9... | collective-permute-start | bytes 786440 | tf_op jit(solution)/shard_map/ppermute | solution.py:26
  78.9 2.7 %collective-permute-done.6.refs_4_ = bf16[512,256]{1,0:T(8,128)(2,1)} collective-permute-done((bf16[512,256]{1,0:T(8,128)(2,1)S(1)}, bf16[512,256]{1,0:T(8,128)(2,1)}, u32[]{:S(2)}, u32[]{:S(2)}) %collective-permute-start.6) | collective-permute-done | bytes 262176 | tf_op jit(solution)/shard_map/ppermute | solution.py:26
  83.0 10.4 %expert.1 = (bf16[8,520,256]{2,1,0:T(8,128)(2,1)}, bf16[8,512,256]{2,1,0:T(8,128)(2,1)}, bf16[176,2048]{1,0:T(8,128)(2,1)}, bf16[176,2048]{1,0:T(8,128)(2,1)}, bf16[176,2048]{1,0:T(8,128)(2,1)}) custom-call(s32[1]{0:T(128)} %bitcast.2.meta, bf16[512,256]{1,0:T(8,128)(2,1)} %bitcast.90, bf16[512,256]{1,0:T(8,128)(2,1)} %copy-done.9, ...), custom_call_target="tpu_custom_call" | custom-call | tf_op jit(solution)/shard_map/expert/pallas_call | solution.py:99
  94.7 4.3 %collective-permute-start.24 = (bf16[512,256]{1,0:T(8,128)(2,1)S(1)}, bf16[512,256]{1,0:T(8,128)(2,1)S(1)}, u32[]{:S(2)}, u32[]{:S(2)}) collective-permute-start(bf16[512,256]{1,0:T(8,128)(2,1)S(1)} %get-tuple-element.29), channel_id=1, source_target_pairs={{0,7},{1,0},{2,1},{3,2},{4,3},{5,4},{6,5},{7,6},{8,15},{9,8},{10,9... | collective-permute-start | bytes 786440 | tf_op jit(solution)/shard_map/ppermute | solution.py:26
  105.0 4.6 %collective-permute-start.25 = (bf16[512,256]{1,0:T(8,128)(2,1)S(1)}, bf16[512,256]{1,0:T(8,128)(2,1)S(1)}, u32[]{:S(2)}, u32[]{:S(2)}) collective-permute-start(bf16[512,256]{1,0:T(8,128)(2,1)S(1)} %fusion.15), channel_id=1, source_target_pairs={{0,7},{1,0},{2,1},{3,2},{4,3},{5,4},{6,5},{7,6},{8,15},{9,8},{10,9... | collective-permute-start | bytes 786440 | tf_op jit(solution)/shard_map/ppermute | solution.py:26
  109.6 3.4 %collective-permute-start.18 = (bf16[520,256]{1,0:T(8,128)(2,1)S(1)}, bf16[520,256]{1,0:T(8,128)(2,1)S(1)}, u32[]{:S(2)}, u32[]{:S(2)}) collective-permute-start(bf16[520,256]{1,0:T(8,128)(2,1)S(1)} %get-tuple-element.23), channel_id=1, source_target_pairs={{0,7},{1,0},{2,1},{3,2},{4,3},{5,4},{6,5},{7,6},{8,15},{9,8},{10,9... | collective-permute-start | bytes 798728 | tf_op jit(solution)/shard_map/ppermute | solution.py:26
  118.1 4.6 %collective-permute-start.26 = (bf16[512,256]{1,0:T(8,128)(2,1)S(1)}, bf16[512,256]{1,0:T(8,128)(2,1)S(1)}, u32[]{:S(2)}, u32[]{:S(2)}) collective-permute-start(bf16[512,256]{1,0:T(8,128)(2,1)S(1)} %get-tuple-element.27), channel_id=1, source_target_pairs={{0,7},{1,0},{2,1},{3,2},{4,3},{5,4},{6,5},{7,6},{8,15},{9,8},{10,9... | collective-permute-start | bytes 786440 | tf_op jit(solution)/shard_map/ppermute | solution.py:26
  124.8 4.7 %collective-permute-start.19 = (bf16[520,256]{1,0:T(8,128)(2,1)S(1)}, bf16[520,256]{1,0:T(8,128)(2,1)S(1)}, u32[]{:S(2)}, u32[]{:S(2)}) collective-permute-start(bf16[520,256]{1,0:T(8,128)(2,1)S(1)} %get-tuple-element.21), channel_id=1, source_target_pairs={{0,7},{1,0},{2,1},{3,2},{4,3},{5,4},{6,5},{7,6},{8,15},{9,8},{10,9... | collective-permute-start | bytes 798728 | tf_op jit(solution)/shard_map/ppermute | solution.py:26
  132.6 4.6 %collective-permute-start.27 = (bf16[512,256]{1,0:T(8,128)(2,1)S(1)}, bf16[512,256]{1,0:T(8,128)(2,1)S(1)}, u32[]{:S(2)}, u32[]{:S(2)}) collective-permute-start(bf16[512,256]{1,0:T(8,128)(2,1)S(1)} %get-tuple-element.25), channel_id=1, source_target_pairs={{0,7},{1,0},{2,1},{3,2},{4,3},{5,4},{6,5},{7,6},{8,15},{9,8},{10,9... | collective-permute-start | bytes 786440 | tf_op jit(solution)/shard_map/ppermute | solution.py:26
  139.3 4.6 %collective-permute-start.20 = (bf16[520,256]{1,0:T(8,128)(2,1)S(1)}, bf16[520,256]{1,0:T(8,128)(2,1)S(1)}, u32[]{:S(2)}, u32[]{:S(2)}) collective-permute-start(bf16[520,256]{1,0:T(8,128)(2,1)S(1)} %get-tuple-element.19), channel_id=1, source_target_pairs={{0,7},{1,0},{2,1},{3,2},{4,3},{5,4},{6,5},{7,6},{8,15},{9,8},{10,9... | collective-permute-start | bytes 798728 | tf_op jit(solution)/shard_map/ppermute | solution.py:26
  143.9 13.6 %collective-permute-start.28 = (bf16[176,2048]{1,0:T(8,128)(2,1)S(1)}, bf16[176,2048]{1,0:T(8,128)(2,1)S(1)}, u32[]{:S(2)}, u32[]{:S(2)}) collective-permute-start(bf16[176,2048]{1,0:T(8,128)(2,1)S(1)} %copy-done.6), channel_id=1, source_target_pairs={{0,256},{256,0},{1,257},{257,1},{2,258},{258,2},{3,259},{259,3},{4... | collective-permute-start | bytes 2162696 | tf_op jit(solution)/shard_map/ppermute | solution.py:156
  159.5 2.4 %collective-permute-start.30 = (bf16[176,2048]{1,0:T(8,128)(2,1)S(1)}, bf16[176,2048]{1,0:T(8,128)(2,1)}, u32[]{:S(2)}, u32[]{:S(2)}) collective-permute-start(bf16[176,2048]{1,0:T(8,128)(2,1)S(1)} %copy-done.4), channel_id=1, source_target_pairs={{0,256},{256,0},{1,257},{257,1},{2,258},{258,2},{3,259},{259,3},{4... | collective-permute-start | bytes 2162696 | tf_op jit(solution)/shard_map/ppermute | solution.py:156
  164.3 4.6 %all-to-all-start.1 = ((bf16[32,40,256]{2,1,0:T(8,128)(2,1)}), bf16[32,40,256]{2,1,0:T(8,128)(2,1)}, u32[]{:S(2)}, u32[]{:S(2)}) async-start(bf16[32,40,256]{2,1,0:T(8,128)(2,1)} %pad_maximum_fusion), calls=%async_computation.1 | async-start | bytes 1310720 | tf_op jit(solution)/shard_map/all_to_all | solution.py:165
  170.0 2.2 %fusion.4 = bf16[1,176,2048]{2,1,0:T(8,128)(2,1)} fusion(bf16[176,2048]{1,0:T(8,128)(2,1)} %collective-permute-done.29, bf16[176,2048]{1,0:T(8,128)(2,1)S(1)} %copy-done.5), kind=kLoop, calls=%fused_computation.11 | loop fusion | flops 1441792 | bytes 2162688 | tf_op jit(solution)/shard_map/broadcast_in_dim | solution.py:157
  172.2 2.2 %fusion.5 = bf16[1,176,2048]{2,1,0:T(8,128)(2,1)} fusion(bf16[176,2048]{1,0:T(8,128)(2,1)} %collective-permute-done.30, bf16[176,2048]{1,0:T(8,128)(2,1)S(1)} %copy-done.4), kind=kLoop, calls=%fused_computation.12 | loop fusion | flops 1441792 | bytes 2162688 | tf_op jit(solution)/shard_map/broadcast_in_dim | solution.py:157
  174.4 13.9 %all-to-all-done.1 = bf16[32,40,256]{2,1,0:T(8,128)(2,1)} async-done(((bf16[32,40,256]{2,1,0:T(8,128)(2,1)}), bf16[32,40,256]{2,1,0:T(8,128)(2,1)}, u32[]{:S(2)}, u32[]{:S(2)}) %all-to-all-start.1) | async-done | bytes 655392 | tf_op jit(solution)/shard_map/all_to_all | solution.py:165
  (119 shorter events, 46.5 us)
Async XLA Ops:
  30.6 17.9 %collective-permute-start.3 = (bf16[512,256]{1,0:T(8,128)(2,1)S(1)}, bf16[512,256]{1,0:T(8,128)(2,1)S(1)}, u32[]{:S(2)}, u32[]{:S(2)}) collective-permute-start(bf16[512,256]{1,0:T(8,128)(2,1)S(1)} %bitcast.88), channel_id=1, source_target_pairs={{0,1},{1,2},{2,3},{3,4},{4,5},{5,6},{6,7},{7,0},{8,9},{9,10},{10,1... | collective-permute-start | bytes 786440 | tf_op jit(solution)/shard_map/ppermute | solution.py:26
  34.6 15.8 %collective-permute-start.7 = (bf16[512,256]{1,0:T(8,128)(2,1)S(1)}, bf16[512,256]{1,0:T(8,128)(2,1)S(1)}, u32[]{:S(2)}, u32[]{:S(2)}) collective-permute-start(bf16[512,256]{1,0:T(8,128)(2,1)S(1)} %bitcast.85), channel_id=1, source_target_pairs={{0,7},{1,0},{2,1},{3,2},{4,3},{5,4},{6,5},{7,6},{8,15},{9,8},{10,9... | collective-permute-start | bytes 786440 | tf_op jit(solution)/shard_map/ppermute | solution.py:26
  46.6 11.9 %collective-permute-start.11 = (bf16[512,256]{1,0:T(8,128)(2,1)S(1)}, bf16[512,256]{1,0:T(8,128)(2,1)S(1)}, u32[]{:S(2)}, u32[]{:S(2)}) collective-permute-start(bf16[512,256]{1,0:T(8,128)(2,1)S(1)} %bitcast.86), channel_id=1, source_target_pairs={{0,1},{1,2},{2,3},{3,4},{4,5},{5,6},{6,7},{7,0},{8,9},{9,10},{10,1... | collective-permute-start | bytes 786440 | tf_op jit(solution)/shard_map/ppermute | solution.py:26
  48.5 11.9 %collective-permute-start.4 = (bf16[512,256]{1,0:T(8,128)(2,1)S(1)}, bf16[512,256]{1,0:T(8,128)(2,1)S(1)}, u32[]{:S(2)}, u32[]{:S(2)}) collective-permute-start(bf16[512,256]{1,0:T(8,128)(2,1)S(1)} %collective-permute-done.3.refs_7_), channel_id=1, source_target_pairs={{0,1},{1,2},{2,3},{3,4},{4,5},{5,6},{6,7},{7,0},{8,9},{9,10},{10,1... | collective-permute-start | bytes 786440 | tf_op jit(solution)/shard_map/ppermute | solution.py:26
  50.5 11.9 %collective-permute-start.8 = (bf16[512,256]{1,0:T(8,128)(2,1)S(1)}, bf16[512,256]{1,0:T(8,128)(2,1)S(1)}, u32[]{:S(2)}, u32[]{:S(2)}) collective-permute-start(bf16[512,256]{1,0:T(8,128)(2,1)S(1)} %collective-permute-done.7.refs_9_), channel_id=1, source_target_pairs={{0,7},{1,0},{2,1},{3,2},{4,3},{5,4},{6,5},{7,6},{8,15},{9,8},{10,9... | collective-permute-start | bytes 786440 | tf_op jit(solution)/shard_map/ppermute | solution.py:26
  55.1 11.9 %collective-permute-start.1 = (bf16[512,256]{1,0:T(8,128)(2,1)S(1)}, bf16[512,256]{1,0:T(8,128)(2,1)S(1)}, u32[]{:S(2)}, u32[]{:S(2)}) collective-permute-start(bf16[512,256]{1,0:T(8,128)(2,1)S(1)} %collective-permute-done.refs_1_), channel_id=1, source_target_pairs={{0,7},{1,0},{2,1},{3,2},{4,3},{5,4},{6,5},{7,6},{8,15},{9,8},{10,9... | collective-permute-start | bytes 786440 | tf_op jit(solution)/shard_map/ppermute | solution.py:26
  58.5 11.9 %collective-permute-start.12 = (bf16[512,256]{1,0:T(8,128)(2,1)S(1)}, bf16[512,256]{1,0:T(8,128)(2,1)S(1)}, u32[]{:S(2)}, u32[]{:S(2)}) collective-permute-start(bf16[512,256]{1,0:T(8,128)(2,1)S(1)} %collective-permute-done.11.refs_15_), channel_id=1, source_target_pairs={{0,1},{1,2},{2,3},{3,4},{4,5},{5,6},{6,7},{7,0},{8,9},{9,10},{10,1... | collective-permute-start | bytes 786440 | tf_op jit(solution)/shard_map/ppermute | solution.py:26
  60.4 11.9 %collective-permute-start.5 = (bf16[512,256]{1,0:T(8,128)(2,1)S(1)}, bf16[512,256]{1,0:T(8,128)(2,1)S(1)}, u32[]{:S(2)}, u32[]{:S(2)}) collective-permute-start(bf16[512,256]{1,0:T(8,128)(2,1)S(1)} %collective-permute-done.4.refs_6_), channel_id=1, source_target_pairs={{0,1},{1,2},{2,3},{3,4},{4,5},{5,6},{6,7},{7,0},{8,9},{9,10},{10,1... | collective-permute-start | bytes 786440 | tf_op jit(solution)/shard_map/ppermute | solution.py:26
  62.4 11.9 %collective-permute-start.9 = (bf16[512,256]{1,0:T(8,128)(2,1)S(1)}, bf16[512,256]{1,0:T(8,128)(2,1)S(1)}, u32[]{:S(2)}, u32[]{:S(2)}) collective-permute-start(bf16[512,256]{1,0:T(8,128)(2,1)S(1)} %collective-permute-done.8.refs_10_), channel_id=1, source_target_pairs={{0,7},{1,0},{2,1},{3,2},{4,3},{5,4},{6,5},{7,6},{8,15},{9,8},{10,9... | collective-permute-start | bytes 786440 | tf_op jit(solution)/shard_map/ppermute | solution.py:26
  67.0 11.9 %collective-permute-start.2 = (bf16[512,256]{1,0:T(8,128)(2,1)S(1)}, bf16[512,256]{1,0:T(8,128)(2,1)S(1)}, u32[]{:S(2)}, u32[]{:S(2)}) collective-permute-start(bf16[512,256]{1,0:T(8,128)(2,1)S(1)} %collective-permute-done.1.refs_2_), channel_id=1, source_target_pairs={{0,7},{1,0},{2,1},{3,2},{4,3},{5,4},{6,5},{7,6},{8,15},{9,8},{10,9... | collective-permute-start | bytes 786440 | tf_op jit(solution)/shard_map/ppermute | solution.py:26
  100.1 12.8 %collective-permute-start.14 = (bf16[520,256]{1,0:T(8,128)(2,1)S(1)}, bf16[520,256]{1,0:T(8,128)(2,1)S(1)}, u32[]{:S(2)}, u32[]{:S(2)}) collective-permute-start(bf16[520,256]{1,0:T(8,128)(2,1)S(1)} %get-tuple-element.22), channel_id=1, source_target_pairs={{0,1},{1,2},{2,3},{3,4},{4,5},{5,6},{6,7},{7,0},{8,9},{9,10},{10,1... | collective-permute-start | bytes 798728 | tf_op jit(solution)/shard_map/ppermute | solution.py:26
  102.0 12.9 %collective-permute-start.21 = (bf16[512,256]{1,0:T(8,128)(2,1)S(1)}, bf16[512,256]{1,0:T(8,128)(2,1)S(1)}, u32[]{:S(2)}, u32[]{:S(2)}) collective-permute-start(bf16[512,256]{1,0:T(8,128)(2,1)S(1)} %get-tuple-element.28), channel_id=1, source_target_pairs={{0,1},{1,2},{2,3},{3,4},{4,5},{5,6},{6,7},{7,0},{8,9},{9,10},{10,1... | collective-permute-start | bytes 786440 | tf_op jit(solution)/shard_map/ppermute | solution.py:26
  109.6 13.1 %collective-permute-start.18 = (bf16[520,256]{1,0:T(8,128)(2,1)S(1)}, bf16[520,256]{1,0:T(8,128)(2,1)S(1)}, u32[]{:S(2)}, u32[]{:S(2)}) collective-permute-start(bf16[520,256]{1,0:T(8,128)(2,1)S(1)} %get-tuple-element.23), channel_id=1, source_target_pairs={{0,7},{1,0},{2,1},{3,2},{4,3},{5,4},{6,5},{7,6},{8,15},{9,8},{10,9... | collective-permute-start | bytes 798728 | tf_op jit(solution)/shard_map/ppermute | solution.py:26
  116.2 13.4 %collective-permute-start.22 = (bf16[512,256]{1,0:T(8,128)(2,1)S(1)}, bf16[512,256]{1,0:T(8,128)(2,1)S(1)}, u32[]{:S(2)}, u32[]{:S(2)}) collective-permute-start(bf16[512,256]{1,0:T(8,128)(2,1)S(1)} %get-tuple-element.26), channel_id=1, source_target_pairs={{0,1},{1,2},{2,3},{3,4},{4,5},{5,6},{6,7},{7,0},{8,9},{9,10},{10,1... | collective-permute-start | bytes 786440 | tf_op jit(solution)/shard_map/ppermute | solution.py:26
  122.8 14.4 %collective-permute-start.16 = (bf16[520,256]{1,0:T(8,128)(2,1)S(1)}, bf16[520,256]{1,0:T(8,128)(2,1)S(1)}, u32[]{:S(2)}, u32[]{:S(2)}) collective-permute-start(bf16[520,256]{1,0:T(8,128)(2,1)S(1)} %get-tuple-element.20), channel_id=1, source_target_pairs={{0,1},{1,2},{2,3},{3,4},{4,5},{5,6},{6,7},{7,0},{8,9},{9,10},{10,1... | collective-permute-start | bytes 798728 | tf_op jit(solution)/shard_map/ppermute | solution.py:26
  124.8 12.4 %collective-permute-start.19 = (bf16[520,256]{1,0:T(8,128)(2,1)S(1)}, bf16[520,256]{1,0:T(8,128)(2,1)S(1)}, u32[]{:S(2)}, u32[]{:S(2)}) collective-permute-start(bf16[520,256]{1,0:T(8,128)(2,1)S(1)} %get-tuple-element.21), channel_id=1, source_target_pairs={{0,7},{1,0},{2,1},{3,2},{4,3},{5,4},{6,5},{7,6},{8,15},{9,8},{10,9... | collective-permute-start | bytes 798728 | tf_op jit(solution)/shard_map/ppermute | solution.py:26
  130.7 26.8 %collective-permute-start.23 = (bf16[512,256]{1,0:T(8,128)(2,1)S(1)}, bf16[512,256]{1,0:T(8,128)(2,1)S(1)}, u32[]{:S(2)}, u32[]{:S(2)}) collective-permute-start(bf16[512,256]{1,0:T(8,128)(2,1)S(1)} %get-tuple-element.24), channel_id=1, source_target_pairs={{0,1},{1,2},{2,3},{3,4},{4,5},{5,6},{6,7},{7,0},{8,9},{9,10},{10,1... | collective-permute-start | bytes 786440 | tf_op jit(solution)/shard_map/ppermute | solution.py:26
  132.6 26.9 %collective-permute-start.27 = (bf16[512,256]{1,0:T(8,128)(2,1)S(1)}, bf16[512,256]{1,0:T(8,128)(2,1)S(1)}, u32[]{:S(2)}, u32[]{:S(2)}) collective-permute-start(bf16[512,256]{1,0:T(8,128)(2,1)S(1)} %get-tuple-element.25), channel_id=1, source_target_pairs={{0,7},{1,0},{2,1},{3,2},{4,3},{5,4},{6,5},{7,6},{8,15},{9,8},{10,9... | collective-permute-start | bytes 786440 | tf_op jit(solution)/shard_map/ppermute | solution.py:26
  137.4 25.6 %collective-permute-start.17 = (bf16[520,256]{1,0:T(8,128)(2,1)S(1)}, bf16[520,256]{1,0:T(8,128)(2,1)S(1)}, u32[]{:S(2)}, u32[]{:S(2)}) collective-permute-start(bf16[520,256]{1,0:T(8,128)(2,1)S(1)} %get-tuple-element.18), channel_id=1, source_target_pairs={{0,1},{1,2},{2,3},{3,4},{4,5},{5,6},{6,7},{7,0},{8,9},{9,10},{10,1... | collective-permute-start | bytes 798728 | tf_op jit(solution)/shard_map/ppermute | solution.py:26
  139.3 23.7 %collective-permute-start.20 = (bf16[520,256]{1,0:T(8,128)(2,1)S(1)}, bf16[520,256]{1,0:T(8,128)(2,1)S(1)}, u32[]{:S(2)}, u32[]{:S(2)}) collective-permute-start(bf16[520,256]{1,0:T(8,128)(2,1)S(1)} %get-tuple-element.19), channel_id=1, source_target_pairs={{0,7},{1,0},{2,1},{3,2},{4,3},{5,4},{6,5},{7,6},{8,15},{9,8},{10,9... | collective-permute-start | bytes 798728 | tf_op jit(solution)/shard_map/ppermute | solution.py:26
  143.9 25.0 %collective-permute-start.28 = (bf16[176,2048]{1,0:T(8,128)(2,1)S(1)}, bf16[176,2048]{1,0:T(8,128)(2,1)S(1)}, u32[]{:S(2)}, u32[]{:S(2)}) collective-permute-start(bf16[176,2048]{1,0:T(8,128)(2,1)S(1)} %copy-done.6), channel_id=1, source_target_pairs={{0,256},{256,0},{1,257},{257,1},{2,258},{258,2},{3,259},{259,3},{4... | collective-permute-start | bytes 2162696 | tf_op jit(solution)/shard_map/ppermute | solution.py:156
  157.5 12.5 %collective-permute-start.29 = (bf16[176,2048]{1,0:T(8,128)(2,1)S(1)}, bf16[176,2048]{1,0:T(8,128)(2,1)}, u32[]{:S(2)}, u32[]{:S(2)}) collective-permute-start(bf16[176,2048]{1,0:T(8,128)(2,1)S(1)} %copy-done.5), channel_id=1, source_target_pairs={{0,256},{256,0},{1,257},{257,1},{2,258},{258,2},{3,259},{259,3},{4... | collective-permute-start | bytes 2162696 | tf_op jit(solution)/shard_map/ppermute | solution.py:156
  159.5 12.7 %collective-permute-start.30 = (bf16[176,2048]{1,0:T(8,128)(2,1)S(1)}, bf16[176,2048]{1,0:T(8,128)(2,1)}, u32[]{:S(2)}, u32[]{:S(2)}) collective-permute-start(bf16[176,2048]{1,0:T(8,128)(2,1)S(1)} %copy-done.4), channel_id=1, source_target_pairs={{0,256},{256,0},{1,257},{257,1},{2,258},{258,2},{3,259},{259,3},{4... | collective-permute-start | bytes 2162696 | tf_op jit(solution)/shard_map/ppermute | solution.py:156
  164.3 24.1 %all-to-all-start.1 = ((bf16[32,40,256]{2,1,0:T(8,128)(2,1)}), bf16[32,40,256]{2,1,0:T(8,128)(2,1)}, u32[]{:S(2)}, u32[]{:S(2)}) async-start(bf16[32,40,256]{2,1,0:T(8,128)(2,1)} %pad_maximum_fusion), calls=%async_computation.1 | async-start | bytes 1310720 | tf_op jit(solution)/shard_map/all_to_all | solution.py:165
  (28 other events, 540.5 us)

commit v2 on v1

v2 whole, which is shorter than its diff:
```python
import jax
import jax.numpy as jnp
from jax import lax
from jax.experimental import pallas as pl
from jax.experimental.pallas import tpu as pltpu
from jax.sharding import PartitionSpec as P


BF = jnp.bfloat16
F32 = jnp.float32
N_T = 8
CAP = 16
FIRST = (4, 5)
REST = (3, 6, 2, 7, 1, 0)


def nt(left, right):
    return lax.dot_general(left, right, (((1,), (1,)), ((), ())), preferred_element_type=F32)


def tn(left, right):
    return lax.dot_general(left, right, (((0,), (0,)), ((), ())), preferred_element_type=F32)


def nn(left, right):
    return lax.dot_general(left, right, (((1,), (0,)), ((), ())), preferred_element_type=F32)


def shift(x, by):
    return lax.ppermute(x, "tensor", [(i, (i + by) % N_T) for i in range(N_T)])


def gather_ring(x, g):
    xs, gs = [x] + [None] * (N_T - 1), [g] + [None] * (N_T - 1)
    half = N_T // 2
    for s in range(1, half + 1):
        xs[-s] = shift(xs[(1 - s) % N_T], 1)
        gs[-s if s < half else s] = shift(gs[(1 - s) % N_T], 1) if s < half else shift(gs[s - 1], -1)
        if s < half:
            xs[s] = shift(xs[s - 1], -1)
            gs[s] = shift(gs[s - 1], -1)
    return xs, gs


def reduce_ring(terms):
    half = N_T // 2
    up, down = terms[half], terms[N_T + 1 - half]
    for s in range(1, half + 1):
        up = shift(up, 1)
        if s < half:
            down = shift(down, -1)
            up = (up.astype(F32) + terms[half - s].astype(F32)).astype(BF)
            if s < half - 1:
                down = (down.astype(F32) + terms[N_T + s + 1 - half].astype(F32)).astype(BF)
    return terms[0], up, down


def iota(shape, dim):
    return lax.broadcasted_iota(jnp.int32, shape, dim)


def call(kernel, out_shape, scalars=0):
    vmem = pl.BlockSpec(memory_space=pltpu.VMEM)

    def run(*args):
        smem = [pl.BlockSpec(memory_space=pltpu.SMEM)] * scalars
        return pl.pallas_call(
            kernel,
            out_shape=out_shape,
            in_specs=smem + [vmem] * (len(args) - scalars),
            out_specs=jax.tree.map(lambda _: vmem, out_shape),
        )(*args)

    return run


def dispatch_kernel(ids, weights, tokens, grads, sent, pick_w):
    experts, twice, width = sent.shape
    cap = twice // 2
    tok_rows = tokens.shape[0]
    choose = ids.shape[0]
    owner = iota((experts, tok_rows), 0)
    named = jnp.zeros((experts, tok_rows), F32)
    weight_et = jnp.zeros((experts, tok_rows), F32)
    for k in range(choose):
        hit = ids[k : k + 1, :] == owner
        named = jnp.where(hit, 1.0, named)
        weight_et = jnp.where(hit, weights[k : k + 1, :], weight_et)
    square = (tok_rows, tok_rows)
    earlier = jnp.where(iota(square, 0) < iota(square, 1), 1.0, 0.0).astype(BF)
    place = jnp.where(named > 0.0, nn(named.astype(BF), earlier), -1.0)
    grid = (experts, cap, tok_rows)
    flat = (experts * cap, tok_rows)
    place = jnp.broadcast_to(place[:, None, :], grid).reshape(flat)
    weight = jnp.broadcast_to(weight_et[:, None, :], grid).reshape(flat)
    slot = (iota(flat, 0) & (cap - 1)).astype(F32)
    chosen = place == slot
    pick = jnp.where(chosen, 1.0, 0.0).astype(BF)
    weight = jnp.where(chosen, weight, 0.0)
    pick_w[...] = weight
    slot_w = jnp.sum(weight, axis=1, keepdims=True)
    rows = nn(pick, tokens[...]).astype(BF)
    scaled = (slot_w * nn(pick, grads[...])).astype(BF)
    sent[:, :cap, :] = rows.reshape(experts, cap, width)
    sent[:, cap:, :] = scaled.reshape(experts, cap, width)


def chunk_cols(meta, width):
    places = [(meta[0] + s) & (N_T - 1) for s in range(N_T)]
    return [pl.ds(pl.multiple_of(at * width, width), width) for at in places]


def side(parts):
    return jnp.concatenate(list(parts), axis=1)


def expert_kernel(meta, *refs):
    xs, gs, refs = refs[:N_T], refs[N_T : 2 * N_T], refs[2 * N_T :]
    wg, wu, wd = refs[:3]
    parts = refs[3:5]
    hidden_ref, gate_ref, up_ref, dots_ref = refs[5:]
    slots, width = xs[0].shape
    blocks = slots // CAP
    cols = chunk_cols(meta, width)

    x = side(r[...] for r in xs)
    gate_value = nt(x, side(wg[:, c] for c in cols))
    up_value = nt(x, side(wu[:, c] for c in cols))
    grad_hidden = nt(side(r[...] for r in gs), side(wd[:, c] for c in cols))
    sigma = jax.nn.sigmoid(gate_value)
    silu = gate_value * sigma
    hidden = (silu * up_value).astype(BF)
    gate_rows = (grad_hidden * up_value * sigma * (1.0 + gate_value * (1.0 - sigma))).astype(BF)
    up_rows = (grad_hidden * silu).astype(BF)
    hidden_ref[...] = hidden
    gate_ref[...] = gate_rows
    up_ref[...] = up_rows

    product = hidden.astype(F32) * grad_hidden
    high = product.astype(BF)
    low = (product - high.astype(F32)).astype(BF)
    ones = jnp.ones((8, product.shape[1]), BF)
    line = (nt(ones, high) + nt(ones, low))[0:1]
    wide, tall = (blocks, slots), (slots, width)
    mine = iota(wide, 1) // CAP == iota(wide, 0)
    spread = jnp.where(mine, line, 0.0).astype(BF)
    place = jnp.where((iota(tall, 0) & (CAP - 1)) == iota(tall, 1), 1.0, 0.0).astype(BF)
    dots = nn(spread, place).astype(BF)
    dots_ref[...] = dots
    for d, part in zip(FIRST, parts):
        write_part(part, hidden, gate_rows, up_rows, dots, wg, wu, wd, cols[d])


def write_part(out, hidden, gate_rows, up_rows, dots, wg, wu, wd, col):
    slots, width = hidden.shape[0], out.shape[1]
    grid = (slots // CAP, CAP, width)
    part = nn(hidden, wd[:, col]).astype(BF)
    gpart = (nn(gate_rows, wg[:, col]) + nn(up_rows, wu[:, col])).astype(BF)
    both = jnp.concatenate([part.reshape(grid), gpart.reshape(grid)], axis=1)
    out[: 2 * slots] = both.reshape(2 * slots, width)
    out[2 * slots :] = dots


def rest_kernel(meta, hidden, gate_rows, up_rows, dots, wg, wu, wd, *parts):
    cols = chunk_cols(meta, parts[0].shape[1])
    for d, part in zip(REST, parts):
        write_part(
            part, hidden[...], gate_rows[...], up_rows[...], dots[...], wg, wu, wd, cols[d]
        )


def grads_kernel(meta, *refs):
    xs, gs = refs[:N_T], refs[N_T : 2 * N_T]
    hidden, gate_rows, up_rows, out = refs[2 * N_T :]
    cols = chunk_cols(meta, xs[0].shape[1])
    hidden_t, gate_t, up_t = hidden[...].T, gate_rows[...].T, up_rows[...].T
    for s in range(N_T):
        out[0, :, cols[s]] = nn(gate_t, xs[s][...]).astype(BF)
        out[1, :, cols[s]] = nn(up_t, xs[s][...]).astype(BF)
        out[2, :, cols[s]] = nn(hidden_t, gs[s][...]).astype(BF)


def pack_kernel(own, up, down, sent):
    experts, _, width = sent.shape
    both = 2 * CAP
    rows = experts * both
    total = own[...].astype(F32) + up[...].astype(F32) + down[...].astype(F32)
    sent[:, :both, :] = total[:rows].astype(BF).reshape(experts, both, width)
    dots = jnp.broadcast_to(total[rows:][:, None, :], (experts, 8, width))
    sent[:, both:, :] = dots.astype(BF)


def combine_kernel(ids, weights, pick_ref, got, layer, grad_tok, grad_w):
    experts, _, width = got.shape
    slots, tok_rows = pick_ref.shape
    cap = slots // experts
    pick_w = pick_ref[...]
    pick = jnp.where(pick_w > 0.0, 1.0, 0.0).astype(BF)
    high = pick_w.astype(BF)
    rest = pick_w - high.astype(F32)
    mid = rest.astype(BF)
    low = (rest - mid.astype(F32)).astype(BF)
    home = got[:, :cap, :].reshape(slots, width)
    layer[...] = (tn(high, home) + tn(mid, home) + tn(low, home)).astype(BF)
    grad_tok[...] = tn(pick, got[:, cap : 2 * cap, :].reshape(slots, width)).astype(BF)
    dots = (0.125 * jnp.sum(got[:, 2 * cap :, :].astype(F32), axis=1)).astype(BF)
    line = (width, slots)
    spread = jnp.where((iota(line, 1) & (cap - 1)) == iota(line, 0), 1.0, 0.0).astype(BF)
    wide = (experts, slots)
    dots = jnp.where(iota(wide, 1) // cap == iota(wide, 0), nn(dots, spread), 0.0).astype(BF)
    dots_et = nn(dots, pick)
    owner = iota((experts, tok_rows), 0)
    for k in range(ids.shape[0]):
        mine = jnp.where(ids[k : k + 1, :] == owner, dots_et, 0.0)
        grad_w[k : k + 1, :] = jnp.sum(mine, axis=0, keepdims=True) / weights[k : k + 1, :]


def body(tokens, expert_ids, route_weights, w_gate, w_up, w_down, out_grad):
    experts = lax.axis_size("expert")
    tok_rows, choose = expert_ids.shape
    width = tokens.shape[1]
    cap = tok_rows * 8 // experts
    slots = experts * cap
    hid = w_gate.shape[1]
    z = lax.axis_index("tensor")
    meta = z.astype(jnp.int32).reshape(1)
    ids, weights = expert_ids.T, route_weights.T

    def shaped(shape, dtype=BF):
        return jax.ShapeDtypeStruct(shape, dtype)

    sent, pick_w = call(
        dispatch_kernel, (shaped((experts, 2 * cap, width)), shaped((slots, tok_rows), F32))
    )(ids, weights, tokens, out_grad)
    got = lax.all_to_all(sent, "expert", split_axis=0, concat_axis=0, tiled=True)
    x0 = got[:, :cap].reshape(slots, width)
    g0 = got[:, cap:].reshape(slots, width)
    xs, gs = gather_ring(x0, g0)

    tall = shaped((2 * slots + experts, width))
    w_args = (w_gate[0], w_up[0], w_down[0])
    made = call(
        expert_kernel,
        (tall,) * 2 + (shaped((slots, hid)),) * 3 + (shaped((experts, width)),),
        scalars=1,
    )(meta, *xs, *gs, *w_args)

    rest = call(rest_kernel, (tall,) * 6, scalars=1)(
        meta, *made[2:], *w_args
    )
    parts = dict(zip(FIRST + REST, made[:2] + rest))
    sums = reduce_ring(parts)
    sent = call(pack_kernel, shaped((experts, 2 * cap + 8, width)))(*sums)
    sent, held = lax.optimization_barrier((sent, made[2:5]))
    got = lax.all_to_all(sent, "expert", split_axis=0, concat_axis=0, tiled=True)
    terms = call(grads_kernel, shaped((3, hid, N_T * width)), scalars=1)(meta, *xs, *gs, *held)
    others = lax.ppermute(terms, "dp", [(0, 1), (1, 0)])
    w_grads = [(terms[i].astype(F32) + others[i].astype(F32)).astype(BF)[None] for i in range(3)]

    layer, grad_tok, grad_w = call(
        combine_kernel,
        (shaped((tok_rows, width)), shaped((tok_rows, width)), shaped((choose, tok_rows), F32)),
    )(ids, weights, pick_w, got)
    return layer, grad_tok, grad_w.T, *w_grads


def solution(mesh):
    placed = (
        P(("dp", "expert"), "tensor"),
        P(("dp", "expert"), None),
        P(("dp", "expert"), None),
        P("expert", "tensor", None),
        P("expert", "tensor", None),
        P("expert", "tensor", None),
        P(("dp", "expert"), "tensor"),
    )
    return jax.shard_map(
        body,
        mesh=mesh,
        in_specs=placed,
        out_specs=(
            P(("dp", "expert"), "tensor"),
            P(("dp", "expert"), "tensor"),
            P(("dp", "expert"), None),
            P("expert", "tensor", None),
            P("expert", "tensor", None),
            P("expert", "tensor", None),
        ),
        check_vma=False,
    )
```

time: 195 us -> 196 us (level)
  the two profiles are of different devices: /device:TPU:1 before, /device:TPU:2 now
where the time goes in v2:
time: 196 us; the launch traced here: 194 us
  starting transfers between devices  78.6 us (40%)
  blocking collectives  54.1 us (28%)
  waiting for transfers between devices  30.4 us (16%)
  Pallas kernels  24.1 us (12%)
  other arithmetic  5.11 us (3%)
    ppermute x21, starting transfers between devices, shift(): return lax.ppermute(x, 'tensor', [(i, (i + by) % N_T) for i in range(N_T)])  76.5 us
    all_to_all x2, blocking collectives, body(): lax.all_to_all(sent, 'expert', split_axis=0, concat_axis=0, tiled=True)  54.1 us
    ppermute x21, waiting for transfers between devices, shift(): return lax.ppermute(x, 'tensor', [(i, (i + by) % N_T) for i in range(N_T)])  30.4 us
    pallas_call x6, Pallas kernels, run(): pl.pallas_call(kernel, out_shape=out_shape, in_specs=smem + [vmem] * (len...  24.1 us
  transfers between devices with their start and end apart: 22, of which 7 were waited for; matrix products, arithmetic and copies ran while one was open for 1% of the time, Pallas kernels for 4%

profile of v2, /device:TPU:2, one launch (start us, length us, event | category | flops | bytes accessed | tf_op | source)
XLA Modules:
  0.0 194.4 jit_solution(8634902787744280766)
XLA Ops:
  2.7 27.1 %all_to_all.10 = bf16[32,32,256]{2,1,0:T(8,128)(2,1)S(1)} all-to-all(bf16[32,32,256]{2,1,0:T(8,128)(2,1)} %get-tuple-element.28), channel_id=1, replica_groups=mesh['dp'=2,'expert'=32,'tensor'=8] {'expert'}, dimensions={0} | all-to-all | bytes 1048576 | tf_op jit(solution)/shard_map/all_to_all | solution.py:235
  29.8 4.3 %collective-permute-start.3 = (bf16[512,256]{1,0:T(8,128)(2,1)S(1)}, bf16[512,256]{1,0:T(8,128)(2,1)S(1)}, u32[]{:S(2)}, u32[]{:S(2)}) collective-permute-start(bf16[512,256]{1,0:T(8,128)(2,1)S(1)} %bitcast.19), channel_id=1, source_target_pairs={{0,1},{1,2},{2,3},{3,4},{4,5},{5,6},{6,7},{7,0},{8,9},{9,10},{10,1... | collective-permute-start | bytes 786440 | tf_op jit(solution)/shard_map/ppermute | solution.py:30
  34.1 8.6 %collective-permute-start.7 = (bf16[512,256]{1,0:T(8,128)(2,1)S(1)}, bf16[512,256]{1,0:T(8,128)(2,1)S(1)}, u32[]{:S(2)}, u32[]{:S(2)}) collective-permute-start(bf16[512,256]{1,0:T(8,128)(2,1)S(1)} %bitcast.15), channel_id=1, source_target_pairs={{0,7},{1,0},{2,1},{3,2},{4,3},{5,4},{6,5},{7,6},{8,15},{9,8},{10,9... | collective-permute-start | bytes 786440 | tf_op jit(solution)/shard_map/ppermute | solution.py:30
  42.7 3.9 %collective-permute-start = (bf16[512,256]{1,0:T(8,128)(2,1)S(1)}, bf16[512,256]{1,0:T(8,128)(2,1)S(1)}, u32[]{:S(2)}, u32[]{:S(2)}) collective-permute-start(bf16[512,256]{1,0:T(8,128)(2,1)S(1)} %bitcast.20), channel_id=1, source_target_pairs={{0,7},{1,0},{2,1},{3,2},{4,3},{5,4},{6,5},{7,6},{8,15},{9,8},{10,9... | collective-permute-start | bytes 786440 | tf_op jit(solution)/shard_map/ppermute | solution.py:30
  50.5 5.1 %collective-permute-start.8 = (bf16[512,256]{1,0:T(8,128)(2,1)S(1)}, bf16[512,256]{1,0:T(8,128)(2,1)S(1)}, u32[]{:S(2)}, u32[]{:S(2)}) collective-permute-start(bf16[512,256]{1,0:T(8,128)(2,1)S(1)} %collective-permute-done.7.refs_9_), channel_id=1, source_target_pairs={{0,7},{1,0},{2,1},{3,2},{4,3},{5,4},{6,5},{7,6},{8,15},{9,8},{10,9... | collective-permute-start | bytes 786440 | tf_op jit(solution)/shard_map/ppermute | solution.py:30
  55.7 3.9 %collective-permute-start.1 = (bf16[512,256]{1,0:T(8,128)(2,1)S(1)}, bf16[512,256]{1,0:T(8,128)(2,1)S(1)}, u32[]{:S(2)}, u32[]{:S(2)}) collective-permute-start(bf16[512,256]{1,0:T(8,128)(2,1)S(1)} %collective-permute-done.refs_1_), channel_id=1, source_target_pairs={{0,7},{1,0},{2,1},{3,2},{4,3},{5,4},{6,5},{7,6},{8,15},{9,8},{10,9... | collective-permute-start | bytes 786440 | tf_op jit(solution)/shard_map/ppermute | solution.py:30
  63.5 5.1 %collective-permute-start.9 = (bf16[512,256]{1,0:T(8,128)(2,1)S(1)}, bf16[512,256]{1,0:T(8,128)(2,1)S(1)}, u32[]{:S(2)}, u32[]{:S(2)}) collective-permute-start(bf16[512,256]{1,0:T(8,128)(2,1)S(1)} %collective-permute-done.8.refs_10_), channel_id=1, source_target_pairs={{0,7},{1,0},{2,1},{3,2},{4,3},{5,4},{6,5},{7,6},{8,15},{9,8},{10,9... | collective-permute-start | bytes 786440 | tf_op jit(solution)/shard_map/ppermute | solution.py:30
  68.7 3.9 %collective-permute-start.2 = (bf16[512,256]{1,0:T(8,128)(2,1)S(1)}, bf16[512,256]{1,0:T(8,128)(2,1)}, u32[]{:S(2)}, u32[]{:S(2)}) collective-permute-start(bf16[512,256]{1,0:T(8,128)(2,1)S(1)} %collective-permute-done.1.refs_2_), channel_id=1, source_target_pairs={{0,7},{1,0},{2,1},{3,2},{4,3},{5,4},{6,5},{7,6},{8,15},{9,8},{10,9... | collective-permute-start | bytes 786440 | tf_op jit(solution)/shard_map/ppermute | solution.py:30
  76.5 5.1 %collective-permute-start.10 = (bf16[512,256]{1,0:T(8,128)(2,1)S(1)}, bf16[512,256]{1,0:T(8,128)(2,1)}, u32[]{:S(2)}, u32[]{:S(2)}) collective-permute-start(bf16[512,256]{1,0:T(8,128)(2,1)S(1)} %collective-permute-done.9.refs_11_), channel_id=1, source_target_pairs={{0,7},{1,0},{2,1},{3,2},{4,3},{5,4},{6,5},{7,6},{8,15},{9,8},{10,9... | collective-permute-start | bytes 786440 | tf_op jit(solution)/shard_map/ppermute | solution.py:30
  82.3 2.8 %collective-permute-done.6.refs_4_ = bf16[512,256]{1,0:T(8,128)(2,1)} collective-permute-done((bf16[512,256]{1,0:T(8,128)(2,1)S(1)}, bf16[512,256]{1,0:T(8,128)(2,1)}, u32[]{:S(2)}, u32[]{:S(2)}) %collective-permute-start.6) | collective-permute-done | bytes 262176 | tf_op jit(solution)/shard_map/ppermute | solution.py:30
  85.6 7.4 %shard_map.119 = (bf16[1056,256]{1,0:T(8,128)(2,1)}, bf16[1056,256]{1,0:T(8,128)(2,1)}, bf16[512,176]{1,0:T(8,128)(2,1)}, bf16[512,176]{1,0:T(8,128)(2,1)}, bf16...) custom-call(s32[1]{0:T(128)} %bitcast.2.meta, bf16[512,256]{1,0:T(8,128)(2,1)} %bitcast.21, bf16[512,256]{1,0:T(8,128)(2,1)} %copy-done.6, ...), custom_call_target="tpu_custom_call" | custom-call | tf_op jit(solution)/shard_map/pallas_call | solution.py:67
  93.0 2.4 %collective-permute-start.14 = (bf16[1056,256]{1,0:T(8,128)(2,1)}, bf16[1056,256]{1,0:T(8,128)(2,1)S(1)}, u32[]{:S(2)}, u32[]{:S(2)}) collective-permute-start(bf16[1056,256]{1,0:T(8,128)(2,1)} %get-tuple-element.34), channel_id=1, source_target_pairs={{0,1},{1,2},{2,3},{3,4},{4,5},{5,6},{6,7},{7,0},{8,9},{9,10},{10,1... | collective-permute-start | bytes 1622024 | tf_op jit(solution)/shard_map/ppermute | solution.py:30
  95.4 5.3 %collective-permute-start.18 = (bf16[1056,256]{1,0:T(8,128)(2,1)}, bf16[1056,256]{1,0:T(8,128)(2,1)S(1)}, u32[]{:S(2)}, u32[]{:S(2)}) collective-permute-start(bf16[1056,256]{1,0:T(8,128)(2,1)} %get-tuple-element.38), channel_id=1, source_target_pairs={{0,7},{1,0},{2,1},{3,2},{4,3},{5,4},{6,5},{7,6},{8,15},{9,8},{10,9... | collective-permute-start | bytes 1622024 | tf_op jit(solution)/shard_map/ppermute | solution.py:30
  100.7 4.9 %shard_map.120 = (bf16[1056,256]{1,0:T(8,128)(2,1)}, bf16[1056,256]{1,0:T(8,128)(2,1)}, bf16[1056,256]{1,0:T(8,128)(2,1)}, bf16[1056,256]{1,0:T(8,128)(2,1)}, bf...) custom-call(s32[1]{0:T(128)} %bitcast.2.meta, bf16[512,176]{1,0:T(8,128)(2,1)} %get-tuple-element.45.hidden.refs_16_, ...), custom_call_target="tpu_custom_call" | custom-call | tf_op jit(solution)/shard_map/pallas_call | solution.py:67
  109.7 5.3 %collective-permute-start.19 = (bf16[1056,256]{1,0:T(8,128)(2,1)S(1)}, bf16[1056,256]{1,0:T(8,128)(2,1)S(1)}, u32[]{:S(2)}, u32[]{:S(2)}) collective-permute-start(bf16[1056,256]{1,0:T(8,128)(2,1)S(1)} %add_convert_fusion.4), channel_id=1, source_target_pairs={{0,7},{1,0},{2,1},{3,2},{4,3},{5,4},{6,5},{7,6},{8,15},{9,8},{10,9... | collective-permute-start | bytes 1622024 | tf_op jit(solution)/shard_map/ppermute | solution.py:30
  115.0 7.1 %collective-permute-done.15 = bf16[1056,256]{1,0:T(8,128)(2,1)S(1)} collective-permute-done((bf16[1056,256]{1,0:T(8,128)(2,1)S(1)}, bf16[1056,256]{1,0:T(8,128)(2,1)S(1)}, u32[]{:S(2)}, u32[]{:S(2)}) %collective-permute-start.15) | collective-permute-done | bytes 540704 | tf_op jit(solution)/shard_map/ppermute | solution.py:30
  122.3 2.7 %collective-permute-start.16 = (bf16[1056,256]{1,0:T(8,128)(2,1)S(1)}, bf16[1056,256]{1,0:T(8,128)(2,1)S(1)}, u32[]{:S(2)}, u32[]{:S(2)}) collective-permute-start(bf16[1056,256]{1,0:T(8,128)(2,1)S(1)} %add_convert_fusion.6), channel_id=1, source_target_pairs={{0,1},{1,2},{2,3},{3,4},{4,5},{5,6},{6,7},{7,0},{8,9},{9,10},{10,1... | collective-permute-start | bytes 1622024 | tf_op jit(solution)/shard_map/ppermute | solution.py:30
  125.2 4.9 %collective-permute-start.20 = (bf16[1056,256]{1,0:T(8,128)(2,1)S(1)}, bf16[1056,256]{1,0:T(8,128)(2,1)S(1)}, u32[]{:S(2)}, u32[]{:S(2)}) collective-permute-start(bf16[1056,256]{1,0:T(8,128)(2,1)S(1)} %add_convert_fusion.3), channel_id=1, source_target_pairs={{0,7},{1,0},{2,1},{3,2},{4,3},{5,4},{6,5},{7,6},{8,15},{9,8},{10,9... | collective-permute-start | bytes 1622024 | tf_op jit(solution)/shard_map/ppermute | solution.py:30
  130.1 8.6 %collective-permute-done.16 = bf16[1056,256]{1,0:T(8,128)(2,1)S(1)} collective-permute-done((bf16[1056,256]{1,0:T(8,128)(2,1)S(1)}, bf16[1056,256]{1,0:T(8,128)(2,1)S(1)}, u32[]{:S(2)}, u32[]{:S(2)}) %collective-permute-start.16) | collective-permute-done | bytes 540704 | tf_op jit(solution)/shard_map/ppermute | solution.py:30
  141.2 10.1 %collective-permute-done.17.up = bf16[1056,256]{1,0:T(8,128)(2,1)S(1)} collective-permute-done((bf16[1056,256]{1,0:T(8,128)(2,1)S(1)}, bf16[1056,256]{1,0:T(8,128)(2,1)S(1)}, u32[]{:S(2)}, u32[]{:S(2)}) %collective-permute-start.17) | collective-permute-done | bytes 540704 | tf_op jit(solution)/shard_map/ppermute | solution.py:30
  152.1 2.4 %shard_map.121 = bf16[32,40,256]{2,1,0:T(8,128)(2,1)} custom-call(bf16[1056,256]{1,0:T(8,128)(2,1)} %get-tuple-element.33.own, bf16[1056,256]{1,0:T(8,128)(2,1)} %copy-done.19, bf16[1056,256]{1,0:T(8,128)(2,1)} %copy-done.18), custom_call_target="tpu_custom_call" | custom-call | tf_op jit(solution)/shard_map/pallas_call | solution.py:67
  154.5 5.1 %shard_map.123 = bf16[3,176,2048]{2,1,0:T(8,128)(2,1)} custom-call(s32[1]{0:T(128)} %bitcast.2.meta, bf16[512,256]{1,0:T(8,128)(2,1)} %bitcast.22, bf16[512,256]{1,0:T(8,128)(2,1)} %copy-done.6, bf16[512,256]{1,0:T(8,128)(2,1)} %copy-done.10, bf16[512,256]{1,0:T(8,128)(2,1)} %collective-permute-done.2.refs_3_, ...), custom_call_target="tpu_custom_call" | custom-call | tf_op jit(solution)/shard_map/pallas_call | solution.py:67
  161.7 27.1 %all_to_all.11.got = bf16[32,40,256]{2,1,0:T(8,128)(2,1)} all-to-all(bf16[32,40,256]{2,1,0:T(8,128)(2,1)S(1)} %copy-done.1), channel_id=1, replica_groups=mesh['dp'=2,'expert'=32,'tensor'=8] {'expert'}, dimensions={0} | all-to-all | bytes 1310720 | tf_op jit(solution)/shard_map/all_to_all | solution.py:255
  191.0 3.4 %add_convert_fusion = (bf16[1,176,2048]{2,1,0:T(8,128)(2,1)}, bf16[1,176,2048]{2,1,0:T(8,128)(2,1)}, bf16[1,176,2048]{2,1,0:T(8,128)(2,1)}) fusion(bf16[3,176,2048]{2,1,0:T(8,128)(2,1)} %collective-permute-done.21, bf16[3,176,2048]{2,1,0:T(8,128)(2,1)S(1)} %copy-done), kind=kLoop, calls=%fused_computation | loop fusion | flops 4325376 | bytes 6488064 | tf_op jit(solution)/shard_map/convert_element_type | solution.py:258
  (75 shorter events, 26.7 us)
Async XLA Ops:
  29.8 55.8 %copy-start.2 = (bf16[32,16,256]{2,1,0:T(8,128)(2,1)}, bf16[32,16,256]{2,1,0:T(8,128)(2,1)S(1)}, u32[]{:S(2)}) copy-start(bf16[32,16,256]{2,1,0:T(8,128)(2,1)S(1)} %get-tuple-element.51) | copy-start | bytes 786436
  29.8 55.8 %copy-start.3 = (bf16[32,16,256]{2,1,0:T(8,128)(2,1)}, bf16[32,16,256]{2,1,0:T(8,128)(2,1)S(1)}, u32[]{:S(2)}) copy-start(bf16[32,16,256]{2,1,0:T(8,128)(2,1)S(1)} %get-tuple-element.52) | copy-start | bytes 786436
  29.8 18.7 %collective-permute-start.3 = (bf16[512,256]{1,0:T(8,128)(2,1)S(1)}, bf16[512,256]{1,0:T(8,128)(2,1)S(1)}, u32[]{:S(2)}, u32[]{:S(2)}) collective-permute-start(bf16[512,256]{1,0:T(8,128)(2,1)S(1)} %bitcast.19), channel_id=1, source_target_pairs={{0,1},{1,2},{2,3},{3,4},{4,5},{5,6},{6,7},{7,0},{8,9},{9,10},{10,1... | collective-permute-start | bytes 786440 | tf_op jit(solution)/shard_map/ppermute | solution.py:30
  34.1 16.4 %collective-permute-start.7 = (bf16[512,256]{1,0:T(8,128)(2,1)S(1)}, bf16[512,256]{1,0:T(8,128)(2,1)S(1)}, u32[]{:S(2)}, u32[]{:S(2)}) collective-permute-start(bf16[512,256]{1,0:T(8,128)(2,1)S(1)} %bitcast.15), channel_id=1, source_target_pairs={{0,7},{1,0},{2,1},{3,2},{4,3},{5,4},{6,5},{7,6},{8,15},{9,8},{10,9... | collective-permute-start | bytes 786440 | tf_op jit(solution)/shard_map/ppermute | solution.py:30
  42.7 13.0 %collective-permute-start = (bf16[512,256]{1,0:T(8,128)(2,1)S(1)}, bf16[512,256]{1,0:T(8,128)(2,1)S(1)}, u32[]{:S(2)}, u32[]{:S(2)}) collective-permute-start(bf16[512,256]{1,0:T(8,128)(2,1)S(1)} %bitcast.20), channel_id=1, source_target_pairs={{0,7},{1,0},{2,1},{3,2},{4,3},{5,4},{6,5},{7,6},{8,15},{9,8},{10,9... | collective-permute-start | bytes 786440 | tf_op jit(solution)/shard_map/ppermute | solution.py:30
  46.6 13.0 %collective-permute-start.11 = (bf16[512,256]{1,0:T(8,128)(2,1)S(1)}, bf16[512,256]{1,0:T(8,128)(2,1)S(1)}, u32[]{:S(2)}, u32[]{:S(2)}) collective-permute-start(bf16[512,256]{1,0:T(8,128)(2,1)S(1)} %bitcast.16), channel_id=1, source_target_pairs={{0,1},{1,2},{2,3},{3,4},{4,5},{5,6},{6,7},{7,0},{8,9},{9,10},{10,1... | collective-permute-start | bytes 786440 | tf_op jit(solution)/shard_map/ppermute | solution.py:30
  48.6 13.0 %collective-permute-start.4 = (bf16[512,256]{1,0:T(8,128)(2,1)S(1)}, bf16[512,256]{1,0:T(8,128)(2,1)S(1)}, u32[]{:S(2)}, u32[]{:S(2)}) collective-permute-start(bf16[512,256]{1,0:T(8,128)(2,1)S(1)} %collective-permute-done.3.refs_7_), channel_id=1, source_target_pairs={{0,1},{1,2},{2,3},{3,4},{4,5},{5,6},{6,7},{7,0},{8,9},{9,10},{10,1... | collective-permute-start | bytes 786440 | tf_op jit(solution)/shard_map/ppermute | solution.py:30
  50.5 13.0 %collective-permute-start.8 = (bf16[512,256]{1,0:T(8,128)(2,1)S(1)}, bf16[512,256]{1,0:T(8,128)(2,1)S(1)}, u32[]{:S(2)}, u32[]{:S(2)}) collective-permute-start(bf16[512,256]{1,0:T(8,128)(2,1)S(1)} %collective-permute-done.7.refs_9_), channel_id=1, source_target_pairs={{0,7},{1,0},{2,1},{3,2},{4,3},{5,4},{6,5},{7,6},{8,15},{9,8},{10,9... | collective-permute-start | bytes 786440 | tf_op jit(solution)/shard_map/ppermute | solution.py:30
  55.7 13.0 %collective-permute-start.1 = (bf16[512,256]{1,0:T(8,128)(2,1)S(1)}, bf16[512,256]{1,0:T(8,128)(2,1)S(1)}, u32[]{:S(2)}, u32[]{:S(2)}) collective-permute-start(bf16[512,256]{1,0:T(8,128)(2,1)S(1)} %collective-permute-done.refs_1_), channel_id=1, source_target_pairs={{0,7},{1,0},{2,1},{3,2},{4,3},{5,4},{6,5},{7,6},{8,15},{9,8},{10,9... | collective-permute-start | bytes 786440 | tf_op jit(solution)/shard_map/ppermute | solution.py:30
  59.6 13.0 %collective-permute-start.12 = (bf16[512,256]{1,0:T(8,128)(2,1)S(1)}, bf16[512,256]{1,0:T(8,128)(2,1)S(1)}, u32[]{:S(2)}, u32[]{:S(2)}) collective-permute-start(bf16[512,256]{1,0:T(8,128)(2,1)S(1)} %collective-permute-done.11.refs_15_), channel_id=1, source_target_pairs={{0,1},{1,2},{2,3},{3,4},{4,5},{5,6},{6,7},{7,0},{8,9},{9,10},{10,1... | collective-permute-start | bytes 786440 | tf_op jit(solution)/shard_map/ppermute | solution.py:30
  61.6 13.0 %collective-permute-start.5 = (bf16[512,256]{1,0:T(8,128)(2,1)S(1)}, bf16[512,256]{1,0:T(8,128)(2,1)S(1)}, u32[]{:S(2)}, u32[]{:S(2)}) collective-permute-start(bf16[512,256]{1,0:T(8,128)(2,1)S(1)} %collective-permute-done.4.refs_6_), channel_id=1, source_target_pairs={{0,1},{1,2},{2,3},{3,4},{4,5},{5,6},{6,7},{7,0},{8,9},{9,10},{10,1... | collective-permute-start | bytes 786440 | tf_op jit(solution)/shard_map/ppermute | solution.py:30
  63.5 13.0 %collective-permute-start.9 = (bf16[512,256]{1,0:T(8,128)(2,1)S(1)}, bf16[512,256]{1,0:T(8,128)(2,1)S(1)}, u32[]{:S(2)}, u32[]{:S(2)}) collective-permute-start(bf16[512,256]{1,0:T(8,128)(2,1)S(1)} %collective-permute-done.8.refs_10_), channel_id=1, source_target_pairs={{0,7},{1,0},{2,1},{3,2},{4,3},{5,4},{6,5},{7,6},{8,15},{9,8},{10,9... | collective-permute-start | bytes 786440 | tf_op jit(solution)/shard_map/ppermute | solution.py:30
  68.7 13.0 %collective-permute-start.2 = (bf16[512,256]{1,0:T(8,128)(2,1)S(1)}, bf16[512,256]{1,0:T(8,128)(2,1)}, u32[]{:S(2)}, u32[]{:S(2)}) collective-permute-start(bf16[512,256]{1,0:T(8,128)(2,1)S(1)} %collective-permute-done.1.refs_2_), channel_id=1, source_target_pairs={{0,7},{1,0},{2,1},{3,2},{4,3},{5,4},{6,5},{7,6},{8,15},{9,8},{10,9... | collective-permute-start | bytes 786440 | tf_op jit(solution)/shard_map/ppermute | solution.py:30
  72.6 9.7 %collective-permute-start.13 = (bf16[512,256]{1,0:T(8,128)(2,1)S(1)}, bf16[512,256]{1,0:T(8,128)(2,1)}, u32[]{:S(2)}, u32[]{:S(2)}) collective-permute-start(bf16[512,256]{1,0:T(8,128)(2,1)S(1)} %collective-permute-done.12.refs_14_), channel_id=1, source_target_pairs={{0,1},{1,2},{2,3},{3,4},{4,5},{5,6},{6,7},{7,0},{8,9},{9,10},{10,1... | collective-permute-start | bytes 786440 | tf_op jit(solution)/shard_map/ppermute | solution.py:30
  74.6 10.5 %collective-permute-start.6 = (bf16[512,256]{1,0:T(8,128)(2,1)S(1)}, bf16[512,256]{1,0:T(8,128)(2,1)}, u32[]{:S(2)}, u32[]{:S(2)}) collective-permute-start(bf16[512,256]{1,0:T(8,128)(2,1)S(1)} %collective-permute-done.5.refs_5_), channel_id=1, source_target_pairs={{0,1},{1,2},{2,3},{3,4},{4,5},{5,6},{6,7},{7,0},{8,9},{9,10},{10,1... | collective-permute-start | bytes 786440 | tf_op jit(solution)/shard_map/ppermute | solution.py:30
  76.5 9.0 %collective-permute-start.10 = (bf16[512,256]{1,0:T(8,128)(2,1)S(1)}, bf16[512,256]{1,0:T(8,128)(2,1)}, u32[]{:S(2)}, u32[]{:S(2)}) collective-permute-start(bf16[512,256]{1,0:T(8,128)(2,1)S(1)} %collective-permute-done.9.refs_11_), channel_id=1, source_target_pairs={{0,7},{1,0},{2,1},{3,2},{4,3},{5,4},{6,5},{7,6},{8,15},{9,8},{10,9... | collective-permute-start | bytes 786440 | tf_op jit(solution)/shard_map/ppermute | solution.py:30
  93.0 13.3 %collective-permute-start.14 = (bf16[1056,256]{1,0:T(8,128)(2,1)}, bf16[1056,256]{1,0:T(8,128)(2,1)S(1)}, u32[]{:S(2)}, u32[]{:S(2)}) collective-permute-start(bf16[1056,256]{1,0:T(8,128)(2,1)} %get-tuple-element.34), channel_id=1, source_target_pairs={{0,1},{1,2},{2,3},{3,4},{4,5},{5,6},{6,7},{7,0},{8,9},{9,10},{10,1... | collective-permute-start | bytes 1622024 | tf_op jit(solution)/shard_map/ppermute | solution.py:30
  95.4 14.1 %collective-permute-start.18 = (bf16[1056,256]{1,0:T(8,128)(2,1)}, bf16[1056,256]{1,0:T(8,128)(2,1)S(1)}, u32[]{:S(2)}, u32[]{:S(2)}) collective-permute-start(bf16[1056,256]{1,0:T(8,128)(2,1)} %get-tuple-element.38), channel_id=1, source_target_pairs={{0,7},{1,0},{2,1},{3,2},{4,3},{5,4},{6,5},{7,6},{8,15},{9,8},{10,9... | collective-permute-start | bytes 1622024 | tf_op jit(solution)/shard_map/ppermute | solution.py:30
  107.5 14.7 %collective-permute-start.15 = (bf16[1056,256]{1,0:T(8,128)(2,1)S(1)}, bf16[1056,256]{1,0:T(8,128)(2,1)S(1)}, u32[]{:S(2)}, u32[]{:S(2)}) collective-permute-start(bf16[1056,256]{1,0:T(8,128)(2,1)S(1)} %add_convert_fusion.7), channel_id=1, source_target_pairs={{0,1},{1,2},{2,3},{3,4},{4,5},{5,6},{6,7},{7,0},{8,9},{9,10},{10,1... | collective-permute-start | bytes 1622024 | tf_op jit(solution)/shard_map/ppermute | solution.py:30
  109.7 15.3 %collective-permute-start.19 = (bf16[1056,256]{1,0:T(8,128)(2,1)S(1)}, bf16[1056,256]{1,0:T(8,128)(2,1)S(1)}, u32[]{:S(2)}, u32[]{:S(2)}) collective-permute-start(bf16[1056,256]{1,0:T(8,128)(2,1)S(1)} %add_convert_fusion.4), channel_id=1, source_target_pairs={{0,7},{1,0},{2,1},{3,2},{4,3},{5,4},{6,5},{7,6},{8,15},{9,8},{10,9... | collective-permute-start | bytes 1622024 | tf_op jit(solution)/shard_map/ppermute | solution.py:30
  122.3 16.4 %collective-permute-start.16 = (bf16[1056,256]{1,0:T(8,128)(2,1)S(1)}, bf16[1056,256]{1,0:T(8,128)(2,1)S(1)}, u32[]{:S(2)}, u32[]{:S(2)}) collective-permute-start(bf16[1056,256]{1,0:T(8,128)(2,1)S(1)} %add_convert_fusion.6), channel_id=1, source_target_pairs={{0,1},{1,2},{2,3},{3,4},{4,5},{5,6},{6,7},{7,0},{8,9},{9,10},{10,1... | collective-permute-start | bytes 1622024 | tf_op jit(solution)/shard_map/ppermute | solution.py:30
  125.2 16.0 %collective-permute-start.20 = (bf16[1056,256]{1,0:T(8,128)(2,1)S(1)}, bf16[1056,256]{1,0:T(8,128)(2,1)S(1)}, u32[]{:S(2)}, u32[]{:S(2)}) collective-permute-start(bf16[1056,256]{1,0:T(8,128)(2,1)S(1)} %add_convert_fusion.3), channel_id=1, source_target_pairs={{0,7},{1,0},{2,1},{3,2},{4,3},{5,4},{6,5},{7,6},{8,15},{9,8},{10,9... | collective-permute-start | bytes 1622024 | tf_op jit(solution)/shard_map/ppermute | solution.py:30
  138.8 12.5 %collective-permute-start.17 = (bf16[1056,256]{1,0:T(8,128)(2,1)S(1)}, bf16[1056,256]{1,0:T(8,128)(2,1)S(1)}, u32[]{:S(2)}, u32[]{:S(2)}) collective-permute-start(bf16[1056,256]{1,0:T(8,128)(2,1)S(1)} %add_convert_fusion.5), channel_id=1, source_target_pairs={{0,1},{1,2},{2,3},{3,4},{4,5},{5,6},{6,7},{7,0},{8,9},{9,10},{10,1... | collective-permute-start | bytes 1622024 | tf_op jit(solution)/shard_map/ppermute | solution.py:30
  159.7 31.4 %collective-permute-start.21 = (bf16[3,176,2048]{2,1,0:T(8,128)(2,1)}, bf16[3,176,2048]{2,1,0:T(8,128)(2,1)}, u32[]{:S(2)}, u32[]{:S(2)}) collective-permute-start(bf16[3,176,2048]{2,1,0:T(8,128)(2,1)} %shard_map.123), channel_id=1, source_target_pairs={{0,256},{256,0},{1,257},{257,1},{2,258},{258,2},{3,259},{259,3},{4... | collective-permute-start | bytes 6488072 | tf_op jit(solution)/shard_map/ppermute | solution.py:257
  (18 other events, 324.0 us)
